TPU v7x, 256 devices: a whole 4x4x8 slice. The times are simulated.
256 devices in a mesh: dp: 4 (over y), expert: 64 (over x, z, core).
Axes of the slice: x: 4, y: 4, z: 8, core: 2. Of those that a mesh axis runs over, the one named last changes fastest.
Arguments:
- tokens: bfloat16 [32768, 2048], P(('dp', 'expert')), may hold values from -6 to 6
- cotangent: bfloat16 [32768, 2048], P(('dp', 'expert')), may hold values from -6 to 6
- expert_ids: int32 [32768, 4], P(('dp', 'expert')), may hold values from 0 to 63, all different within a row; in each aligned block of 128 rows (0 to 127, 128 to 255, ...) at most 10 rows name the same one
- gate_probs: bfloat16 [32768, 4], P(('dp', 'expert')), may hold values from 0.049804688 to 1
- w_gate: bfloat16 [64, 2048, 512], P('expert', 'dp'), may hold values from -0.125 to 0.125
- w_up: bfloat16 [64, 2048, 512], P('expert', 'dp'), may hold values from -0.125 to 0.125
- w_down: bfloat16 [64, 512, 2048], P('expert', None, 'dp'), may hold values from -0.25 to 0.25
Outputs:
- mixed: bfloat16 [32768, 2048], P(('dp', 'expert'))
- grad_tokens: bfloat16 [32768, 2048], P(('dp', 'expert'))
- grad_gates: float32 [32768, 4], P(('dp', 'expert'))
- grad_gate_w: float32 [64, 2048, 512], P('expert', 'dp')
- grad_up_w: float32 [64, 2048, 512], P('expert', 'dp')
- grad_down_w: float32 [64, 512, 2048], P('expert', None, 'dp')
Inputs may be any that keep to these rules, and one draw needn't show every extreme that they name: `expert_ids`: each row names 4 different experts. Within the rows of one device (aligned blocks of 128 rows) no expert is named by more than 10 rows, a bound that some block reaches.
All inputs are finite; a program needn't handle non-finite values.
Results may differ from a plain program's by a relative error of at most 0.0085.
Values may be sent and summed in bfloat16 or wider, within the bound.
No kernel may reach another device: no remote copies, remote signals or barrier semaphores. Data moves between devices by JAX's collectives and lax.ppermute only.
A program may use at most 128 MiB of HBM per device.

v0:
```python
import jax
import jax.numpy as jnp
from jax import lax
from jax.sharding import PartitionSpec as P


def silu_parts(pre_gate):
    sigma = jax.nn.sigmoid(pre_gate)
    return (pre_gate * sigma, sigma * (1.0 + pre_gate * (1.0 - sigma)))


def on_device(tokens, cotangent, expert_ids, gate_probs, w_gate, w_up, w_down):
    axis_count = lax.axis_size("expert")
    local_experts = w_gate.shape[0]
    tok_rows = tokens.shape[0]
    model_width = tokens.shape[1]
    top_count = expert_ids.shape[1]
    all_experts = local_experts * axis_count
    capacity = max(2, 5 * tok_rows * top_count // (4 * all_experts))
    pair_count = tok_rows * top_count
    flat_ids = expert_ids.reshape(-1)
    onehot = (flat_ids[:, None] == jnp.arange(all_experts, dtype=jnp.int32)[None, :]).astype(
        jnp.int32
    )
    earlier = jnp.cumsum(onehot, axis=0) - onehot
    slot_rank = jnp.sum(earlier * onehot, axis=1)
    position = flat_ids * capacity + slot_rank
    pair_table = jnp.full((all_experts * capacity,), pair_count, jnp.int32)
    pair_table = pair_table.at[position].set(jnp.arange(pair_count, dtype=jnp.int32))
    routed = (
        gate_probs.astype(jnp.float32)[:, :, None] * cotangent.astype(jnp.float32)[:, None, :]
    ).astype(jnp.bfloat16)
    routed = routed.reshape(pair_count, model_width)
    send_shape = (axis_count, local_experts, capacity, model_width)
    token_send = jnp.take(
        tokens, pair_table // top_count, axis=0, mode="fill", fill_value=0
    ).reshape(send_shape)
    routed_send = jnp.take(routed, pair_table, axis=0, mode="fill", fill_value=0).reshape(
        send_shape
    )
    token_recv, routed_recv = (
        lax.all_to_all(token_send, "expert", split_axis=0, concat_axis=2, tiled=True),
        lax.all_to_all(routed_send, "expert", split_axis=0, concat_axis=2, tiled=True),
    )
    rows_in = token_recv[0]
    routed_in = routed_recv[0]
    full_gate, full_up, full_down = (
        lax.all_gather(w_gate, "dp", axis=1, tiled=True),
        lax.all_gather(w_up, "dp", axis=1, tiled=True),
        lax.all_gather(w_down, "dp", axis=2, tiled=True),
    )
    pre_gate = jnp.einsum("end,edf->enf", rows_in, full_gate, preferred_element_type=jnp.float32)
    pre_up = jnp.einsum("end,edf->enf", rows_in, full_up, preferred_element_type=jnp.float32)
    activated, slope = silu_parts(pre_gate)
    hidden = (activated * pre_up).astype(jnp.bfloat16)
    expert_out = jnp.einsum(
        "enf,efd->end", hidden, full_down, preferred_element_type=jnp.float32
    ).astype(jnp.bfloat16)
    grad_hidden = jnp.einsum(
        "end,efd->enf", routed_in, full_down, preferred_element_type=jnp.float32
    )
    grad_pre_gate = (grad_hidden * pre_up * slope).astype(jnp.bfloat16)
    grad_pre_up = (grad_hidden * activated).astype(jnp.bfloat16)
    pair_grad = jnp.einsum(
        "enf,edf->end", grad_pre_gate, full_gate, preferred_element_type=jnp.float32
    )
    pair_grad = pair_grad + jnp.einsum(
        "enf,edf->end", grad_pre_up, full_up, preferred_element_type=jnp.float32
    )
    pair_grad = pair_grad.astype(jnp.bfloat16)
    back_out, back_grad = (
        lax.all_to_all(expert_out[None], "expert", split_axis=2, concat_axis=0, tiled=True),
        lax.all_to_all(pair_grad[None], "expert", split_axis=2, concat_axis=0, tiled=True),
    )
    out_pairs = back_out.reshape(all_experts * capacity, model_width)[position].reshape(
        tok_rows, top_count, model_width
    )
    grad_pairs = back_grad.reshape(all_experts * capacity, model_width)[position].reshape(
        tok_rows, top_count, model_width
    )
    mixed = jnp.einsum(
        "tk,tkd->td", gate_probs, out_pairs, preferred_element_type=jnp.float32
    ).astype(jnp.bfloat16)
    grad_gates = jnp.einsum("td,tkd->tk", cotangent, out_pairs, preferred_element_type=jnp.float32)
    grad_tokens = jnp.sum(grad_pairs.astype(jnp.float32), axis=1).astype(jnp.bfloat16)
    part_gate = jnp.einsum(
        "end,enf->edf", rows_in, grad_pre_gate, preferred_element_type=jnp.float32
    )
    part_up = jnp.einsum("end,enf->edf", rows_in, grad_pre_up, preferred_element_type=jnp.float32)
    part_down = jnp.einsum("enf,end->efd", hidden, routed_in, preferred_element_type=jnp.float32)
    grad_gate_w, grad_up_w, grad_down_w = (
        lax.psum_scatter(
            part_gate.astype(jnp.bfloat16), "dp", scatter_dimension=1, tiled=True
        ).astype(jnp.float32),
        lax.psum_scatter(
            part_up.astype(jnp.bfloat16), "dp", scatter_dimension=1, tiled=True
        ).astype(jnp.float32),
        lax.psum_scatter(
            part_down.astype(jnp.bfloat16), "dp", scatter_dimension=2, tiled=True
        ).astype(jnp.float32),
    )
    return (mixed, grad_tokens, grad_gates, grad_gate_w, grad_up_w, grad_down_w)


def solution(mesh):
    in_specs = (
        P(("dp", "expert"), None),
        P(("dp", "expert"), None),
        P(("dp", "expert"), None),
        P(("dp", "expert"), None),
        P("expert", "dp", None),
        P("expert", "dp", None),
        P("expert", None, "dp"),
    )
    out_specs = (
        P(("dp", "expert"), None),
        P(("dp", "expert"), None),
        P(("dp", "expert"), None),
        P("expert", "dp", None),
        P("expert", "dp", None),
        P("expert", None, "dp"),
    )
    return jax.shard_map(
        on_device, mesh=mesh, in_specs=in_specs, out_specs=out_specs, check_vma=False
    )
```

profile of v0, /device:TPU:1, one launch (start us, length us, event | category | flops | bytes accessed | tf_op | source)
XLA Modules:
  0.0 483.9 jit_solution(13898282972535384496)
XLA Ops:
  19.7 4.5 select_bitcast_fusion.1
  24.2 13.3 %all-to-all-start = ((bf16[64,1,10,2048]{3,2,1,0:T(8,128)(2,1)}), bf16[64,1,10,2048]{3,2,1,0:T(8,128)(2,1)}, u32[]{:S(2)}, u32[]{:S(2)}) async-start(bf16[64,1,10,2048]{3,2,1,0:T(8,128)(2,1)} %select_bitcast_fusion.1), calls=%async_computation | async-start | bytes 8388608 | tf_op jit(solution)/shard_map/all_to_all | solution.py:42
  42.2 5.3 %mul.77 = f32[512,2048]{1,0:T(8,128)} reshape(f32[128,4,2048]{2,1,0:T(4,128)} %mul.76) | data formatting | bytes 8388608 | tf_op jit(solution)/shard_map/mul | solution.py:31
  50.3 4.1 gather_fusion.2
  54.4 5.4 %gather.22 = bf16[64,1,10,2048]{3,2,0,1:T(8,128)(2,1)} reshape(bf16[640,2048]{1,0:T(8,128)(2,1)} %gather_fusion.2) | data formatting | bytes 5242880 | tf_op jit(solution)/shard_map/jit(_take)/gather | solution.py:38
  59.8 4.5 select_bitcast_fusion
  64.3 69.0 %all-to-all-done = bf16[64,1,10,2048]{3,2,1,0:T(8,128)(2,1)} async-done(((bf16[64,1,10,2048]{3,2,1,0:T(8,128)(2,1)}), bf16[64,1,10,2048]{3,2,1,0:T(8,128)(2,1)}, u32[]{:S(2)}, u32[]{:S(2)}) %all-to-all-start) | async-done | bytes 2621472 | tf_op jit(solution)/shard_map/all_to_all | solution.py:42
  133.3 5.9 %all-to-all-start.2 = ((bf16[64,1,10,2048]{3,2,1,0:T(8,128)(2,1)}), bf16[64,1,10,2048]{3,2,1,0:T(8,128)(2,1)}, u32[]{:S(2)}, u32[]{:S(2)}) async-start(bf16[64,1,10,2048]{3,2,1,0:T(8,128)(2,1)} %select_bitcast_fusion), calls=%async_computation.2 | async-start | bytes 8388608 | tf_op jit(solution)/shard_map/all_to_all | solution.py:43
  140.0 5.5 %reshape.213 = bf16[640,2048]{1,0:T(8,128)(2,1)} reshape(bf16[64,1,10,2048]{3,2,1,0:T(8,128)(2,1)} %all-to-all-done) | data formatting | bytes 5242880 | tf_op jit(solution)/shard_map/reshape.7
  145.6 89.5 %all-to-all-done.2 = bf16[64,1,10,2048]{3,2,1,0:T(8,128)(2,1)} async-done(((bf16[64,1,10,2048]{3,2,1,0:T(8,128)(2,1)}), bf16[64,1,10,2048]{3,2,1,0:T(8,128)(2,1)}, u32[]{:S(2)}, u32[]{:S(2)}) %all-to-all-start.2) | async-done | bytes 2621472 | tf_op jit(solution)/shard_map/all_to_all | solution.py:43
  235.1 4.3 reshape.219
  239.4 5.0 %fusion.13 = f32[640,512]{1,0:T(8,128)} fusion(bf16[640,2048]{1,0:T(8,128)(2,1)} %reshape.213, bf16[1,2048,512]{2,1,0:T(8,128)(2,1)} %all-gather.4.cloned.1.call-done), kind=kOutput, calls=%fused_computation.28 | convolution fusion | flops 1342177280 | bytes 6029312 | tf_op jit(solution)/shard_map/end,edf->enf/dot_general | solution.py:52
  244.4 5.0 %fusion.9 = f32[640,512]{1,0:T(8,128)} fusion(bf16[640,2048]{1,0:T(8,128)(2,1)} %reshape.213, bf16[1,2048,512]{2,1,0:T(8,128)(2,1)} %all-gather.6.cloned.1.call-done), kind=kOutput, calls=%fused_computation.24 | convolution fusion | flops 1342177280 | bytes 6029312 | tf_op jit(solution)/shard_map/end,edf->enf/dot_general | solution.py:53
  249.3 5.5 %multiply_convert_fusion.1 = (bf16[640,512]{1,0:T(8,128)(2,1)}, bf16[640,512]{1,0:T(8,128)(2,1)S(1)}, bf16[640,512]{1,0:T(8,128)(2,1)}) fusion(f32[640,512]{1,0:T(8,128)} %fusion.13, f32[640,512]{1,0:T(8,128)} %fusion.9, bf16[640,2048]{1,0:T(8,128)(2,1)S(1)} %reshape.219, bf16[1,512,2048]{2,1,0:T(8,128)(2,1)} %all-gather.8.cloned.1.call-done), kind=kOutput, calls=%fused_computation.30 | convolution fusion | flops 1347092480 | bytes 9306112 | tf_op jit(solution)/shard_map/end,efd->enf/dot_general | solution.py:59
  265.5 8.1 %copy.54 = bf16[1,1,640,2048]{3,1,0,2:T(2,128)(2,1)} copy(bf16[1,1,640,2048]{3,2,1,0:T(8,128)(2,1)} %fusion.1) | data formatting | bytes 5242880 | tf_op jit(solution)/shard_map/broadcast_in_dim | solution.py:73
  274.2 17.7 %reduce.4 = bf16[640,2048]{1,0:T(8,128)(2,1)} reduce(bf16[640,1,1,2048]{3,2,1,0:T(2,128)(2,1)} %bitcast.89, bf16[]{:T(256)} %broadcast.135), dimensions={1,2}, to_apply=%bitcast.85.reduce_sub_computation | reduce | bytes 5242882
  291.9 5.2 %reshape.274 = bf16[64,2,10240]{2,1,0:T(2,128)(2,1)} reshape(bf16[640,2048]{1,0:T(8,128)(2,1)} %reduce.4) | data formatting | bytes 5242880
  297.1 5.9 %all-to-all-start.3 = ((bf16[64,2,10240]{2,1,0:T(2,128)(2,1)}), bf16[64,2,10240]{2,1,0:T(2,128)(2,1)}, u32[]{:S(2)}, u32[]{:S(2)}) async-start(bf16[64,2,10240]{2,1,0:T(2,128)(2,1)} %reshape.274), calls=%async_computation.3 | async-start | bytes 5242880 | tf_op jit(solution)/shard_map/all_to_all | solution.py:73
  303.0 5.0 %fusion.3 = bf16[1,2048,512]{2,1,0:T(8,128)(2,1)} fusion(bf16[640,2048]{1,0:T(8,128)(2,1)} %reshape.213, bf16[640,512]{1,0:T(8,128)(2,1)} %get-tuple-element.8), kind=kOutput, calls=%fused_computation.16 | convolution fusion | flops 1343225856 | bytes 5373952 | tf_op jit(solution)/shard_map/end,enf->edf/dot_general | solution.py:89
  308.1 4.8 fusion
  312.9 8.1 %copy.55 = bf16[1,1,640,2048]{3,1,0,2:T(2,128)(2,1)} copy(bf16[1,1,640,2048]{3,2,1,0:T(8,128)(2,1)} %fusion) | data formatting | bytes 5242880 | tf_op jit(solution)/shard_map/broadcast_in_dim | solution.py:72
  321.0 17.9 %reduce.3 = bf16[640,2048]{1,0:T(8,128)(2,1)} reduce(bf16[640,1,1,2048]{3,2,1,0:T(2,128)(2,1)} %bitcast.90, bf16[]{:T(256)} %broadcast.135), dimensions={1,2}, to_apply=%bitcast.86.reduce_sub_computation | reduce | bytes 5242882
  338.9 5.2 %reshape.272 = bf16[64,2,10240]{2,1,0:T(2,128)(2,1)} reshape(bf16[640,2048]{1,0:T(8,128)(2,1)} %reduce.3) | data formatting | bytes 5242880
  344.1 21.1 %all-to-all-done.3 = bf16[64,2,10240]{2,1,0:T(2,128)(2,1)} async-done(((bf16[64,2,10240]{2,1,0:T(2,128)(2,1)}), bf16[64,2,10240]{2,1,0:T(2,128)(2,1)}, u32[]{:S(2)}, u32[]{:S(2)}) %all-to-all-start.3) | async-done | bytes 2621472 | tf_op jit(solution)/shard_map/all_to_all | solution.py:73
  365.2 5.9 %all-to-all-start.1 = ((bf16[64,2,10240]{2,1,0:T(2,128)(2,1)}), bf16[64,2,10240]{2,1,0:T(2,128)(2,1)}, u32[]{:S(2)}, u32[]{:S(2)}) async-start(bf16[64,2,10240]{2,1,0:T(2,128)(2,1)} %reshape.272), calls=%async_computation.1 | async-start | bytes 5242880 | tf_op jit(solution)/shard_map/all_to_all | solution.py:72
  371.1 4.2 fusion.4
  379.9 29.0 %reduce-scatter.8.cloned.1.call-done = bf16[1,512,512]{2,1,0:T(8,128)(2,1)} async-done(((bf16[1,512,2048]{2,1,0:T(8,128)(2,1)}), bf16[1,512,512]{2,1,0:T(8,128)(2,1)}) %reduce-scatter.8.cloned.1.call-update) | async-done | bytes 524304 | tf_op jit(solution)/shard_map/reduce_scatter | solution.py:98
  411.0 16.3 %reshape.275 = bf16[640,1,1,2048]{3,2,1,0:T(2,128)(2,1)} reshape(bf16[64,2,10240]{2,1,0:T(2,128)(2,1)} %all-to-all-done.3) | data formatting | bytes 5242880
  427.3 4.1 copy.51
  434.7 4.1 reshape.221
  438.8 16.3 %reshape.273 = bf16[640,1,1,2048]{3,2,1,0:T(2,128)(2,1)} reshape(bf16[64,2,10240]{2,1,0:T(2,128)(2,1)} %all-to-all-done.1) | data formatting | bytes 5242880
  467.8 4.6 fusion.16
  (84 shorter events, 58.9 us)
Async XLA Ops:
  7.2 6.1 %copy-start = (bf16[128,2048]{1,0:T(8,128)(2,1)S(1)}, bf16[128,2048]{1,0:T(8,128)(2,1)}, u32[]{:S(2)}) copy-start(bf16[128,2048]{1,0:T(8,128)(2,1)} %param.7) | copy-start | bytes 1572868
  24.1 14.9 %copy-start.8 = (bf16[128,2048]{1,0:T(8,128)(2,1)S(1)}, bf16[128,2048]{1,0:T(8,128)(2,1)}, u32[]{:S(2)}) copy-start(bf16[128,2048]{1,0:T(8,128)(2,1)} %param.8) | copy-start | bytes 1572868
  24.2 109.2 %all-to-all-start = ((bf16[64,1,10,2048]{3,2,1,0:T(8,128)(2,1)}), bf16[64,1,10,2048]{3,2,1,0:T(8,128)(2,1)}, u32[]{:S(2)}, u32[]{:S(2)}) async-start(bf16[64,1,10,2048]{3,2,1,0:T(8,128)(2,1)} %select_bitcast_fusion.1), calls=%async_computation | async-start | bytes 8388608 | tf_op jit(solution)/shard_map/all_to_all | solution.py:42
  37.5 201.9 %all-gather.4.cloned.1.call-start = ((), (), s32[]{:S(2)}) async-start(), calls=%async_computation.7 | async-start | bytes 2621440 | tf_op jit(solution)/shard_map/all_gather | solution.py:48
  38.2 206.2 %all-gather.6.cloned.1.call-start = ((), (), s32[]{:S(2)}) async-start(), calls=%async_computation.8 | async-start | bytes 2621440 | tf_op jit(solution)/shard_map/all_gather | solution.py:49
  42.2 5.3 %copy-start.10 = (bf16[128,4]{0,1:T(4,128)(2,1)S(1)}, bf16[128,4]{0,1:T(4,128)(2,1)}, u32[]{:S(2)}) copy-start(bf16[128,4]{0,1:T(4,128)(2,1)} %param.10) | copy-start | bytes 3076
  133.3 101.8 %all-to-all-start.2 = ((bf16[64,1,10,2048]{3,2,1,0:T(8,128)(2,1)}), bf16[64,1,10,2048]{3,2,1,0:T(8,128)(2,1)}, u32[]{:S(2)}, u32[]{:S(2)}) async-start(bf16[64,1,10,2048]{3,2,1,0:T(8,128)(2,1)} %select_bitcast_fusion), calls=%async_computation.2 | async-start | bytes 8388608 | tf_op jit(solution)/shard_map/all_to_all | solution.py:43
  139.2 110.1 %all-gather.8.cloned.1.call-start = ((), (), s32[]{:S(2)}) async-start(), calls=%async_computation.9 | async-start | bytes 2621440 | tf_op jit(solution)/shard_map/all_gather | solution.py:50
  140.0 235.6 %reduce-scatter.4.cloned.1.call-start = ((), (), s32[]{:S(2)}) async-start(), calls=%async_computation.10 | async-start | bytes 2621440 | tf_op jit(solution)/shard_map/reduce_scatter | solution.py:92
  249.3 6.4 %copy-start.3 = (bf16[640,2048]{1,0:T(8,128)(2,1)S(1)}, bf16[640,2048]{1,0:T(8,128)(2,1)}, u32[]{:S(2)}) copy-start(bf16[640,2048]{1,0:T(8,128)(2,1)} %reshape.213) | copy-start | bytes 7864324
  254.9 0.8 copy-start.6
  258.9 3.5 copy-start.5
  258.9 3.5 copy-start.7
  297.1 68.0 %all-to-all-start.3 = ((bf16[64,2,10240]{2,1,0:T(2,128)(2,1)}), bf16[64,2,10240]{2,1,0:T(2,128)(2,1)}, u32[]{:S(2)}, u32[]{:S(2)}) async-start(bf16[64,2,10240]{2,1,0:T(2,128)(2,1)} %reshape.274), calls=%async_computation.3 | async-start | bytes 5242880 | tf_op jit(solution)/shard_map/all_to_all | solution.py:73
  303.0 74.7 %reduce-scatter.6.cloned.1.call-start = ((), (), s32[]{:S(2)}) async-start(), calls=%async_computation.11 | async-start | bytes 2621440 | tf_op jit(solution)/shard_map/reduce_scatter | solution.py:95
  365.2 73.7 %all-to-all-start.1 = ((bf16[64,2,10240]{2,1,0:T(2,128)(2,1)}), bf16[64,2,10240]{2,1,0:T(2,128)(2,1)}, u32[]{:S(2)}, u32[]{:S(2)}) async-start(bf16[64,2,10240]{2,1,0:T(2,128)(2,1)} %reshape.272), calls=%async_computation.1 | async-start | bytes 5242880 | tf_op jit(solution)/shard_map/all_to_all | solution.py:72
  371.1 37.8 %reduce-scatter.8.cloned.1.call-start = ((), (), s32[]{:S(2)}) async-start(), calls=%async_computation.12 | async-start | bytes 2621440 | tf_op jit(solution)/shard_map/reduce_scatter | solution.py:98
  465.4 2.4 copy-start.4
  465.4 2.3 copy-start.9
  467.8 5.3 %copy-start.2 = (bf16[128,4,2048]{2,1,0:T(4,128)(2,1)S(1)}, bf16[128,4,2048]{2,1,0:T(4,128)(2,1)}, u32[]{:S(2)}) copy-start(bf16[128,4,2048]{2,1,0:T(4,128)(2,1)} %reshape.221) | copy-start | bytes 6291460
  467.8 9.1 %copy-start.1 = (bf16[128,2048]{1,0:T(8,128)(2,1)S(1)}, bf16[128,2048]{1,0:T(8,128)(2,1)}, u32[]{:S(2)}) copy-start(bf16[128,2048]{1,0:T(8,128)(2,1)} %param.7) | copy-start | bytes 1572868
Sparse Core Ops, SparseCore 0:
  40.1 34.3 all-gather.3
  76.2 33.3 all-gather.5
  141.9 34.3 all-gather.7
  259.0 28.8 reduce-scatter.3
  308.2 33.3 reduce-scatter.5
  375.5 33.3 reduce-scatter.7
where the time goes:
time: 493 us; the launch traced here: 484 us
  waiting for transfers between devices  211 us (43%)
  local copies, waits for them, and re-layouts  123 us (25%)
  other arithmetic  59.6 us (12%)
  matrix products  45.1 us (9%)
  starting transfers between devices  31.2 us (6%)
  between operations  14.6 us (3%)
    all_to_all x1, waiting for transfers between devices, on_device(): lax.all_to_all(routed_send, 'expert', split_axis=0, concat_axis=2, tiled=...  89.5 us
    all_to_all x1, waiting for transfers between devices, on_device(): lax.all_to_all(token_send, 'expert', split_axis=0, concat_axis=2, tiled=T...  69 us
    unnamed x31, local copies, waits for them, and re-layouts  53.5 us
    unnamed x2, other arithmetic  35.6 us
    reduce_scatter x1, waiting for transfers between devices, on_device(): lax.psum_scatter(part_down.astype(jnp.bfloat16), 'dp', scatter_dimension=...  29 us
    all_to_all x1, waiting for transfers between devices, on_device(): lax.all_to_all(pair_grad[None], 'expert', split_axis=2, concat_axis=0, ti...  21.1 us
    all_to_all x1, starting transfers between devices, on_device(): lax.all_to_all(token_send, 'expert', split_axis=0, concat_axis=2, tiled=T...  13.3 us
  transfers between devices with their start and end apart: 10, of which 4 were waited for; matrix products, arithmetic and copies ran while one was open for 34% of the time, Pallas kernels for 0%

commit v1 on v0

v1 whole, which is shorter than its diff:
```python
import functools

import jax
import jax.numpy as jnp
from jax import lax
from jax.experimental import pallas as pl
from jax.experimental.pallas import tpu as pltpu
from jax.sharding import PartitionSpec as P


INTERPRET = False
LANES = 128


def smem():
    return pl.BlockSpec(memory_space=pltpu.SMEM)


def vmem():
    return pl.BlockSpec(memory_space=pltpu.VMEM)


def clear_rows(out_ref, step=16):
    rows = out_ref.shape[0]
    zero = jnp.zeros((step,) + out_ref.shape[1:], out_ref.dtype)

    def body(i, carry):
        out_ref[pl.ds(i * step, step)] = zero
        return carry

    lax.fori_loop(0, rows // step, body, 0)


def route_kernel(top, capacity, ids_ref, tok_ref, out_ref, pos_ref, count_ref):
    def reset(i, carry):
        count_ref[i] = 0
        return carry

    lax.fori_loop(0, count_ref.shape[0], reset, 0)
    clear_rows(out_ref)

    def body(t, carry):
        row = tok_ref[t]
        names = [ids_ref[top * t + k] for k in range(top)]
        slots = [count_ref[e] for e in names]
        for k in range(top):
            count_ref[names[k]] = slots[k] + 1
            place = names[k] * capacity + slots[k]
            pos_ref[top * t + k] = place
            out_ref[place] = row
        return carry

    lax.fori_loop(0, tok_ref.shape[0], body, 0)


def weigh_kernel(top, pos_ref, gate_ref, cot_ref, out_ref):
    clear_rows(out_ref)

    def body(t, carry):
        row = cot_ref[t].astype(jnp.float32)
        for k in range(top):
            out_ref[pos_ref[top * t + k]] = (row * gate_ref[top * t + k]).astype(jnp.bfloat16)
        return carry

    lax.fori_loop(0, cot_ref.shape[0], body, 0)


def mix_kernel(top, pos_ref, gate_ref, cot_ref, back_ref, mixed_ref, dots_ref):
    def body(t, carry):
        cot = cot_ref[t].astype(jnp.float32)
        total = jnp.zeros(cot.shape, jnp.float32)
        for k in range(top):
            row = back_ref[pos_ref[top * t + k]].astype(jnp.float32)
            total = total + row * gate_ref[top * t + k]
            dots_ref[pl.ds(top * t + k, 1), :] = jnp.sum(row * cot, axis=0, keepdims=True)
        mixed_ref[t] = total.astype(jnp.bfloat16)
        return carry

    lax.fori_loop(0, cot_ref.shape[0], body, 0)


def gather_sum_kernel(top, pos_ref, back_ref, out_ref):
    def body(t, carry):
        total = back_ref[pos_ref[top * t]].astype(jnp.float32)
        for k in range(1, top):
            total = total + back_ref[pos_ref[top * t + k]].astype(jnp.float32)
        out_ref[t] = total.astype(jnp.bfloat16)
        return carry

    lax.fori_loop(0, out_ref.shape[0], body, 0)


def silu_parts(pre_gate):
    sigma = jax.nn.sigmoid(pre_gate)
    return (pre_gate * sigma, sigma * (1.0 + pre_gate * (1.0 - sigma)))


def to_rows(wire, width):
    return wire.reshape(-1, width)


def to_wire(rows, sublanes):
    return rows.reshape(-1, sublanes, LANES)


def on_device(tokens, cotangent, expert_ids, gate_probs, w_gate, w_up, w_down):
    group = lax.axis_size("expert")
    all_experts = w_gate.shape[0] * group
    rows, width = tokens.shape
    top = expert_ids.shape[1]
    capacity = max(2, 5 * rows * top // (4 * all_experts))
    slots = all_experts * capacity
    sub = width // LANES
    f32, bf16 = jnp.float32, jnp.bfloat16

    def exchange(x):
        chunks = x.reshape(group, capacity * sub, LANES)
        return lax.all_to_all(chunks, "expert", 0, 0, tiled=True).reshape(slots, sub, LANES)

    wire_shape = jax.ShapeDtypeStruct((slots, sub, LANES), bf16)
    token_shape = jax.ShapeDtypeStruct((rows, sub, LANES), bf16)
    params = pltpu.CompilerParams(vmem_limit_bytes=32 << 20)
    call = functools.partial(pl.pallas_call, compiler_params=params, interpret=INTERPRET)

    flat_ids = expert_ids.reshape(-1)
    gates = gate_probs.astype(f32).reshape(-1)
    token_tiles = to_wire(tokens, sub)
    cot_tiles = to_wire(cotangent, sub)

    token_send, position = call(
        functools.partial(route_kernel, top, capacity),
        out_shape=(wire_shape, jax.ShapeDtypeStruct((rows * top,), jnp.int32)),
        in_specs=[smem(), vmem()],
        out_specs=(vmem(), smem()),
        scratch_shapes=[pltpu.SMEM((all_experts,), jnp.int32)],
        name="route",
    )(flat_ids, token_tiles)
    token_recv = exchange(token_send)

    routed_send = call(
        functools.partial(weigh_kernel, top),
        out_shape=wire_shape,
        in_specs=[smem(), smem(), vmem()],
        out_specs=vmem(),
        name="weigh",
    )(position, gates, cot_tiles)
    routed_recv = exchange(routed_send)

    full_gate = lax.all_gather(w_gate[0], "dp", axis=0, tiled=True)
    full_up = lax.all_gather(w_up[0], "dp", axis=0, tiled=True)
    full_down = lax.all_gather(w_down[0], "dp", axis=1, tiled=True)

    def dot(a, b, dims):
        return lax.dot_general(a, b, (dims, ((), ())), preferred_element_type=f32)

    rows_in = to_rows(token_recv, width)
    pre_gate = dot(rows_in, full_gate, ((1,), (0,)))
    pre_up = dot(rows_in, full_up, ((1,), (0,)))
    activated, _ = silu_parts(pre_gate)
    hidden = (activated * pre_up).astype(bf16)
    expert_out = dot(hidden, full_down, ((1,), (0,))).astype(bf16)
    out_send = to_wire(expert_out, sub)
    back_out = exchange(out_send)

    routed_recv, pre_gate, pre_up, _ = lax.optimization_barrier(
        (routed_recv, pre_gate, pre_up, out_send)
    )
    activated, slope = silu_parts(pre_gate)
    routed_in = to_rows(routed_recv, width)
    grad_hidden = dot(routed_in, full_down, ((1,), (1,)))
    grad_pre_gate = (grad_hidden * pre_up * slope).astype(bf16)
    grad_pre_up = (grad_hidden * activated).astype(bf16)
    pair_grad = dot(grad_pre_gate, full_gate, ((1,), (1,)))
    pair_grad = (pair_grad + dot(grad_pre_up, full_up, ((1,), (1,)))).astype(bf16)
    grad_send = to_wire(pair_grad, sub)
    back_grad = exchange(grad_send)

    def weight_part(a, b):
        return dot(a, b, ((0,), (0,))).astype(bf16)

    def reduce_weight(part, axis):
        return lax.psum_scatter(part, "dp", scatter_dimension=axis, tiled=True).astype(f32)[None]

    grad_down_w = reduce_weight(weight_part(hidden, routed_in), 1)
    grad_gate_w = reduce_weight(weight_part(rows_in, grad_pre_gate), 0)
    grad_up_w = reduce_weight(weight_part(rows_in, grad_pre_up), 0)

    mixed, dots = call(
        functools.partial(mix_kernel, top),
        out_shape=(token_shape, jax.ShapeDtypeStruct((rows * top, LANES), f32)),
        in_specs=[smem(), smem(), vmem(), vmem()],
        out_specs=(vmem(), vmem()),
        name="mix",
    )(position, gates, cot_tiles, back_out)
    grad_gates = jnp.sum(dots, axis=1).reshape(rows, top)

    grad_tokens = call(
        functools.partial(gather_sum_kernel, top),
        out_shape=token_shape,
        in_specs=[smem(), vmem()],
        out_specs=vmem(),
        name="gather_sum",
    )(position, back_grad)
    return (
        to_rows(mixed, width),
        to_rows(grad_tokens, width),
        grad_gates,
        grad_gate_w,
        grad_up_w,
        grad_down_w,
    )


def solution(mesh):
    tokens = P(("dp", "expert"), None)
    first = P("expert", "dp", None)
    last = P("expert", None, "dp")

    return jax.shard_map(
        on_device,
        mesh=mesh,
        in_specs=(tokens, tokens, tokens, tokens, first, first, last),
        out_specs=(tokens, tokens, tokens, first, first, last),
        check_vma=False,
    )
```

time: 493 us -> 318 us (0.65); the launches traced: 484 us -> 317 us
  local copies, waits for them, and re-layouts: 123 us -> 18.6 us
  other arithmetic: 59.6 us -> 6.58 us
  waiting for transfers between devices: 211 us -> 192 us
  Pallas kernels: 0 us -> 15.1 us
  matrix products: 45.1 us -> 39.5 us
    unnamed x31 -> x20, local copies, waits for them, and re-layouts: 53.5 us -> 5.39 us
    unnamed x2 -> x0, other arithmetic: 35.6 us -> none
    gather x6 -> x0, local copies, waits for them, and re-layouts: 22.3 us -> none  [the longest x2 9.51 us: on_device(): jnp.take(routed, pair_table, axis=0, mode='fill', fill_value=0)]
    all_to_all x4, waiting for transfers between devices: 180 us -> 160 us  [exchange(): lax.all_to_all(chunks, 'expert', 0, 0, tiled=True)]
    broadcast_in_dim x4 -> x0, local copies, waits for them, and re-layouts: 16.5 us -> none  [the longest x1 8.12 us: on_device(): pair_grad[None]]
    pallas_call x0 -> x4, Pallas kernels: none -> 15.1 us  [the longest x1 5.25 us: on_device(): call(functools.partial(route_kernel, top, capacity), out_shape=(wire_shap...]
    select_n x4 -> x0, other arithmetic: 9.05 us -> none  [the longest x2 4.55 us: on_device(): jnp.take(routed, pair_table, axis=0, mode='fill', fill_value=0)]
    convert_element_type x5 -> x0, other arithmetic: 8.92 us -> none  [the longest x3 6.43 us: on_device(): grad_gate_w, grad_up_w, grad_down_w = (lax.psum_scatter(part_gate.astype(...]
  transfers between devices with their start and end apart: 10 -> 10, of which waited for: 4 -> 5; matrix products, arithmetic and copies ran while one was open for 34% -> 19% of each run, Pallas kernels for 0% -> 2%
where the time goes in v1:
time: 318 us; the launch traced here: 317 us
  waiting for transfers between devices  192 us (60%)
  matrix products  39.5 us (12%)
  starting transfers between devices  30.9 us (10%)
  local copies, waits for them, and re-layouts  18.6 us (6%)
  Pallas kernels  15.1 us (5%)
  between operations  14.3 us (4%)
  other arithmetic  6.58 us (2%)
    all_to_all x4, waiting for transfers between devices, exchange(): lax.all_to_all(chunks, 'expert', 0, 0, tiled=True)  160 us
    dot_general x9, matrix products, dot(): return lax.dot_general(a, b, (dims, ((), ())), preferred_element_type=f32)  39.5 us
    all_to_all x4, starting transfers between devices, exchange(): lax.all_to_all(chunks, 'expert', 0, 0, tiled=True)  30.5 us
    reduce_scatter x3, waiting for transfers between devices, reduce_weight(): lax.psum_scatter(part, 'dp', scatter_dimension=axis, tiled=True).astype(f32)  29.2 us
    another operation x2, local copies, waits for them, and re-layouts, exchange(): chunks = x.reshape(group, capacity * sub, LANES)  8.41 us
    broadcast_in_dim x3, other arithmetic, reduce_weight(): lax.psum_scatter(part, 'dp', scatter_dimension=axis, tiled=True).astype(f32)  6.43 us
  transfers between devices with their start and end apart: 10, of which 5 were waited for; matrix products, arithmetic and copies ran while one was open for 19% of the time, Pallas kernels for 2%

profile of v1, /device:TPU:1, one launch (start us, length us, event | category | flops | bytes accessed | tf_op | source)
XLA Modules:
  0.0 316.8 jit_solution(14302666631768910113)
XLA Ops:
  8.1 1.1 copy.16
  9.2 5.2 %route.1 = (bf16[640,16,128]{2,1,0:T(8,128)(2,1)}, s32[512]{0:T(512)S(1)}) custom-call(s32[512]{0:T(512)S(1)} %reshape.54.ids_ref, bf16[128,16,128]{2,1,0:T(8,128)(2,1)S(1)} %bitcast.64), custom_call_target="tpu_custom_call" | custom-call | tf_op jit(solution)/shard_map/route/pallas_call | solution.py:130
  14.5 13.0 %all-to-all-start = ((bf16[64,160,128]{2,1,0:T(8,128)(2,1)}), bf16[64,160,128]{2,1,0:T(8,128)(2,1)S(1)}, u32[]{:S(2)}, u32[]{:S(2)}) async-start(bf16[64,160,128]{2,1,0:T(8,128)(2,1)} %bitcast), calls=%async_computation | async-start | bytes 5242880 | tf_op jit(solution)/shard_map/all_to_all | solution.py:118
  29.2 1.1 copy.17
  30.4 3.8 %weigh.1 = bf16[640,16,128]{2,1,0:T(8,128)(2,1)} custom-call(s32[512]{0:T(512)S(1)} %get-tuple-element.13.pos_ref, f32[512]{0:T(512)S(1)} %reshape.69.gate_ref, bf16[128,16,128]{2,1,0:T(8,128)(2,1)S(1)} %bitcast.62), custom_call_target="tpu_custom_call" | custom-call | tf_op jit(solution)/shard_map/weigh/pallas_call | solution.py:140
  34.2 55.5 %all-to-all-done = bf16[64,160,128]{2,1,0:T(8,128)(2,1)S(1)} async-done(((bf16[64,160,128]{2,1,0:T(8,128)(2,1)}), bf16[64,160,128]{2,1,0:T(8,128)(2,1)S(1)}, u32[]{:S(2)}, u32[]{:S(2)}) %all-to-all-start) | async-done | bytes 2621472 | tf_op jit(solution)/shard_map/all_to_all | solution.py:118
  89.7 5.9 %all-to-all-start.2 = ((bf16[64,160,128]{2,1,0:T(8,128)(2,1)}), bf16[64,160,128]{2,1,0:T(8,128)(2,1)}, u32[]{:S(2)}, u32[]{:S(2)}) async-start(bf16[64,160,128]{2,1,0:T(8,128)(2,1)} %bitcast.5), calls=%async_computation.2 | async-start | bytes 5242880 | tf_op jit(solution)/shard_map/all_to_all | solution.py:118
  96.4 3.1 reshape_reshape.9
  99.5 5.1 %fusion.12 = f32[640,512]{1,0:T(8,128)} fusion(bf16[640,2048]{1,0:T(8,128)(2,1)} %reshape_reshape.9, bf16[1,2048,512]{2,1,0:T(8,128)(2,1)} %all-gather.7.cloned.1.call-done), kind=kOutput, calls=%fused_computation.17 | convolution fusion | flops 1342177280 | bytes 6029312 | tf_op jit(solution)/shard_map/dot_general | solution.py:154
  104.6 4.8 %multiply_convert_fusion.2 = (bf16[640,512]{1,0:T(8,128)(2,1)}, f32[640,512]{1,0:T(8,128)}) fusion(f32[640,512]{1,0:T(8,128)} %fusion.12, bf16[640,2048]{1,0:T(8,128)(2,1)S(1)} %copy-done.2, bf16[1,2048,512]{2,1,0:T(8,128)(2,1)} %all-gather.9.cloned.1.call-done), kind=kOutput, calls=%fused_computation.22 | convolution fusion | flops 1344143360 | bytes 7995392 | tf_op jit(solution)/shard_map/dot_general | solution.py:154
  109.4 48.4 %all-to-all-done.2 = bf16[64,160,128]{2,1,0:T(8,128)(2,1)} async-done(((bf16[64,160,128]{2,1,0:T(8,128)(2,1)}), bf16[64,160,128]{2,1,0:T(8,128)(2,1)}, u32[]{:S(2)}, u32[]{:S(2)}) %all-to-all-start.2) | async-done | bytes 2621472 | tf_op jit(solution)/shard_map/all_to_all | solution.py:118
  157.8 5.2 %convolution_convert_fusion.1 = bf16[512,2048]{1,0:T(8,128)(2,1)} fusion(bf16[640,512]{1,0:T(8,128)(2,1)} %get-tuple-element.28, bf16[80,8,16,128]{3,2,1,0:T(8,128)(2,1)} %bitcast.20), kind=kOutput, calls=%fused_computation.2 | convolution fusion | flops 1343225856 | bytes 5373952 | tf_op jit(solution)/shard_map/dot_general | solution.py:154
  163.0 3.3 %convolution_convert_fusion = bf16[640,2048]{1,0:T(8,128)(2,1)S(1)} fusion(bf16[640,512]{1,0:T(8,128)(2,1)} %get-tuple-element.28, bf16[1,512,2048]{2,1,0:T(8,128)(2,1)} %all-gather.11.cloned.1.call-done), kind=kOutput, calls=%fused_computation.1 | convolution fusion | flops 1343488000 | bytes 5373952 | tf_op jit(solution)/shard_map/dot_general | solution.py:154
  166.3 3.2 reshape_reshape.10
  169.5 5.7 %all-to-all-start.1 = ((bf16[64,160,128]{2,1,0:T(8,128)(2,1)}), bf16[64,160,128]{2,1,0:T(8,128)(2,1)S(1)}, u32[]{:S(2)}, u32[]{:S(2)}) async-start(bf16[64,160,128]{2,1,0:T(8,128)(2,1)} %reshape_reshape.10), calls=%async_computation.1 | async-start | bytes 5242880 | tf_op jit(solution)/shard_map/all_to_all | solution.py:118
  175.5 6.2 %multiply_convert_fusion = (bf16[640,512]{1,0:T(8,128)(2,1)S(1)}, bf16[640,512]{1,0:T(8,128)(2,1)}) fusion(f32[640,512]{1,0:T(8,128)} %fusion.12, f32[640,512]{1,0:T(8,128)} %get-tuple-element.17, bf16[1,512,2048]{2,1,0:T(8,128)(2,1)} %all-gather.11.cloned.1.call-done, bf16[80,8,16,128]{3,2,1,0:T(8,128)(2,1)} %bitcast.20), kind=kOutput, calls=%fused_computation.19 | convolution fusion | flops 1346437120 | bytes 8650752 | tf_op jit(solution)/shard_map/dot_general | solution.py:154
  181.7 0.8 copy-done.5
  182.5 3.2 %convolution_convert_fusion.2 = bf16[2048,512]{1,0:T(8,128)(2,1)} fusion(bf16[640,2048]{1,0:T(8,128)(2,1)S(1)} %copy-done.3, bf16[640,512]{1,0:T(8,128)(2,1)S(1)} %get-tuple-element.26), kind=kOutput, calls=%fused_computation.3 | convolution fusion | flops 1343225856 | bytes 5373952 | tf_op jit(solution)/shard_map/dot_general | solution.py:154
  185.7 3.5 %fusion.10 = f32[640,2048]{1,0:T(8,128)S(1)} fusion(bf16[640,512]{1,0:T(8,128)(2,1)} %get-tuple-element.27, bf16[1,2048,512]{2,1,0:T(8,128)(2,1)} %all-gather.7.cloned.1.call-done), kind=kOutput, calls=%fused_computation.15 | convolution fusion | flops 1342177280 | bytes 7995392 | tf_op jit(solution)/shard_map/dot_general | solution.py:154
  189.2 3.1 add_convert_fusion
  192.4 5.3 %reshape_reshape.11 = bf16[64,160,128]{2,1,0:T(8,128)(2,1)} reshape(bf16[640,2048]{1,0:T(8,128)(2,1)} %add_convert_fusion) | data formatting | bytes 5242880 | tf_op jit(solution)/shard_map/reshape;reshape | solution.py:117
  197.6 39.8 %all-to-all-done.1 = bf16[64,160,128]{2,1,0:T(8,128)(2,1)S(1)} async-done(((bf16[64,160,128]{2,1,0:T(8,128)(2,1)}), bf16[64,160,128]{2,1,0:T(8,128)(2,1)S(1)}, u32[]{:S(2)}, u32[]{:S(2)}) %all-to-all-start.1) | async-done | bytes 2621472 | tf_op jit(solution)/shard_map/all_to_all | solution.py:118
  237.5 5.9 %all-to-all-start.3 = ((bf16[64,160,128]{2,1,0:T(8,128)(2,1)}), bf16[64,160,128]{2,1,0:T(8,128)(2,1)}, u32[]{:S(2)}, u32[]{:S(2)}) async-start(bf16[64,160,128]{2,1,0:T(8,128)(2,1)} %reshape_reshape.11), calls=%async_computation.3 | async-start | bytes 5242880 | tf_op jit(solution)/shard_map/all_to_all | solution.py:118
  243.4 5.1 %convolution_convert_fusion.3 = bf16[2048,512]{1,0:T(8,128)(2,1)} fusion(bf16[640,2048]{1,0:T(8,128)(2,1)} %reshape_reshape.9, bf16[640,512]{1,0:T(8,128)(2,1)} %get-tuple-element.27), kind=kOutput, calls=%fused_computation.4 | convolution fusion | flops 1343225856 | bytes 5373952 | tf_op jit(solution)/shard_map/dot_general | solution.py:154
  248.6 2.1 bitcast_convert_fusion
  250.7 2.1 bitcast_convert_fusion.1
  252.9 29.2 %reduce-scatter.4.cloned.1.call-done = bf16[512,512]{1,0:T(8,128)(2,1)} async-done(((bf16[2048,512]{1,0:T(8,128)(2,1)}), bf16[512,512]{1,0:T(8,128)(2,1)}) %reduce-scatter.4.cloned.1.call-update) | async-done | bytes 524304 | tf_op jit(solution)/shard_map/reduce_scatter | solution.py:182
  282.1 2.1 bitcast_convert_fusion.2
  284.2 2.9 mix.1
  288.8 16.7 %all-to-all-done.3 = bf16[64,160,128]{2,1,0:T(8,128)(2,1)} async-done(((bf16[64,160,128]{2,1,0:T(8,128)(2,1)}), bf16[64,160,128]{2,1,0:T(8,128)(2,1)}, u32[]{:S(2)}, u32[]{:S(2)}) %all-to-all-start.3) | async-done | bytes 2621472 | tf_op jit(solution)/shard_map/all_to_all | solution.py:118
  305.5 3.2 gather_sum.1
  308.7 1.2 copy_bitcast_fusion
  (39 shorter events, 5.4 us)
Async XLA Ops:
  14.5 14.5 %copy-start.7 = (bf16[128,4]{0,1:T(4,128)(2,1)S(1)}, bf16[128,4]{0,1:T(4,128)(2,1)}, u32[]{:S(2)}) copy-start(bf16[128,4]{0,1:T(4,128)(2,1)} %param.10) | copy-start | bytes 3076
  14.5 75.2 %all-to-all-start = ((bf16[64,160,128]{2,1,0:T(8,128)(2,1)}), bf16[64,160,128]{2,1,0:T(8,128)(2,1)S(1)}, u32[]{:S(2)}, u32[]{:S(2)}) async-start(bf16[64,160,128]{2,1,0:T(8,128)(2,1)} %bitcast), calls=%async_computation | async-start | bytes 5242880 | tf_op jit(solution)/shard_map/all_to_all | solution.py:118
  27.5 72.0 %all-gather.7.cloned.1.call-start = ((), (), s32[]{:S(2)}) async-start(), calls=%async_computation.10 | async-start | bytes 2621440 | tf_op jit(solution)/shard_map/all_gather | solution.py:149
  28.2 76.4 %all-gather.9.cloned.1.call-start = ((), (), s32[]{:S(2)}) async-start(), calls=%async_computation.11 | async-start | bytes 2621440 | tf_op jit(solution)/shard_map/all_gather | solution.py:150
  89.7 68.1 %all-to-all-start.2 = ((bf16[64,160,128]{2,1,0:T(8,128)(2,1)}), bf16[64,160,128]{2,1,0:T(8,128)(2,1)}, u32[]{:S(2)}, u32[]{:S(2)}) async-start(bf16[64,160,128]{2,1,0:T(8,128)(2,1)} %bitcast.5), calls=%async_computation.2 | async-start | bytes 5242880 | tf_op jit(solution)/shard_map/all_to_all | solution.py:118
  95.6 67.4 %all-gather.11.cloned.1.call-start = ((), (), s32[]{:S(2)}) async-start(), calls=%async_computation.12 | async-start | bytes 2621440 | tf_op jit(solution)/shard_map/all_gather | solution.py:151
  96.4 152.2 %reduce-scatter.8.cloned.1.call-start = ((), (), s32[]{:S(2)}) async-start(), calls=%async_computation.9 | async-start | bytes 2621440 | tf_op jit(solution)/shard_map/reduce_scatter | solution.py:182
  99.5 5.1 %copy-start.2 = (bf16[640,2048]{1,0:T(8,128)(2,1)S(1)}, bf16[640,2048]{1,0:T(8,128)(2,1)}, u32[]{:S(2)}) copy-start(bf16[640,2048]{1,0:T(8,128)(2,1)} %reshape_reshape.9) | copy-start | bytes 7864324
  169.5 68.0 %all-to-all-start.1 = ((bf16[64,160,128]{2,1,0:T(8,128)(2,1)}), bf16[64,160,128]{2,1,0:T(8,128)(2,1)S(1)}, u32[]{:S(2)}, u32[]{:S(2)}) async-start(bf16[64,160,128]{2,1,0:T(8,128)(2,1)} %reshape_reshape.10), calls=%async_computation.1 | async-start | bytes 5242880 | tf_op jit(solution)/shard_map/all_to_all | solution.py:118
  175.2 75.5 %reduce-scatter.6.cloned.1.call-start = ((), (), s32[]{:S(2)}) async-start(), calls=%async_computation.8 | async-start | bytes 2621440 | tf_op jit(solution)/shard_map/reduce_scatter | solution.py:182
  175.5 7.0 %copy-start.3 = (bf16[640,2048]{1,0:T(8,128)(2,1)S(1)}, bf16[640,2048]{1,0:T(8,128)(2,1)}, u32[]{:S(2)}) copy-start(bf16[640,2048]{1,0:T(8,128)(2,1)} %reshape_reshape.9) | copy-start | bytes 7864324
  181.7 0.8 copy-start.5
  185.7 3.5 %copy-start.4 = (bf16[1,2048,512]{2,1,0:T(8,128)(2,1)S(1)}, bf16[1,2048,512]{2,1,0:T(8,128)(2,1)}, u32[]{:S(2)}) copy-start(bf16[1,2048,512]{2,1,0:T(8,128)(2,1)} %all-gather.9.cloned.1.call-done) | copy-start | bytes 6291460
  185.7 3.5 %copy-start.6 = (bf16[640,512]{1,0:T(8,128)(2,1)S(1)}, bf16[640,512]{1,0:T(8,128)(2,1)}, u32[]{:S(2)}) copy-start(bf16[640,512]{1,0:T(8,128)(2,1)} %copy-done.5) | copy-start | bytes 1966084
  237.5 68.1 %all-to-all-start.3 = ((bf16[64,160,128]{2,1,0:T(8,128)(2,1)}), bf16[64,160,128]{2,1,0:T(8,128)(2,1)}, u32[]{:S(2)}, u32[]{:S(2)}) async-start(bf16[64,160,128]{2,1,0:T(8,128)(2,1)} %reshape_reshape.11), calls=%async_computation.3 | async-start | bytes 5242880 | tf_op jit(solution)/shard_map/all_to_all | solution.py:118
  243.4 38.7 %reduce-scatter.4.cloned.1.call-start = ((), (), s32[]{:S(2)}) async-start(), calls=%async_computation.7 | async-start | bytes 2621440 | tf_op jit(solution)/shard_map/reduce_scatter | solution.py:182
  287.1 0.8 copy-start
  287.9 20.8 %copy-start.1 = (bf16[128,16,128]{2,1,0:T(8,128)(2,1)S(1)}, bf16[128,16,128]{2,1,0:T(8,128)(2,1)}, u32[]{:S(2)}) copy-start(bf16[128,16,128]{2,1,0:T(8,128)(2,1)} %copy-done) | copy-start | bytes 1572868
Sparse Core Ops, SparseCore 0:
  30.1 34.3 all-gather.6
  66.3 33.3 all-gather.8
  101.5 33.3 all-gather.10
  163.1 28.7 reduce-scatter.7
  194.3 32.0 reduce-scatter.5
  248.7 33.3 reduce-scatter.3

commit v2 on v1

--- a/solution.py
+++ b/solution.py
@@ -41,12 +41,12 @@
 
     def body(t, carry):
         row = tok_ref[t]
-        names = [ids_ref[top * t + k] for k in range(top)]
+        names = [ids_ref[k, t] for k in range(top)]
         slots = [count_ref[e] for e in names]
         for k in range(top):
             count_ref[names[k]] = slots[k] + 1
             place = names[k] * capacity + slots[k]
-            pos_ref[top * t + k] = place
+            pos_ref[k, t] = place
             out_ref[place] = row
         return carry
 
@@ -59,20 +59,22 @@
     def body(t, carry):
         row = cot_ref[t].astype(jnp.float32)
         for k in range(top):
-            out_ref[pos_ref[top * t + k]] = (row * gate_ref[top * t + k]).astype(jnp.bfloat16)
+            out_ref[pos_ref[k, t]] = (row * gate_ref[k, t]).astype(jnp.bfloat16)
         return carry
 
     lax.fori_loop(0, cot_ref.shape[0], body, 0)
 
 
 def mix_kernel(top, pos_ref, gate_ref, cot_ref, back_ref, mixed_ref, dots_ref):
+    rows = cot_ref.shape[0]
+
     def body(t, carry):
         cot = cot_ref[t].astype(jnp.float32)
         total = jnp.zeros(cot.shape, jnp.float32)
         for k in range(top):
-            row = back_ref[pos_ref[top * t + k]].astype(jnp.float32)
-            total = total + row * gate_ref[top * t + k]
-            dots_ref[pl.ds(top * t + k, 1), :] = jnp.sum(row * cot, axis=0, keepdims=True)
+            row = back_ref[pos_ref[k, t]].astype(jnp.float32)
+            total = total + row * gate_ref[k, t]
+            dots_ref[pl.ds(k * rows + t, 1), :] = jnp.sum(row * cot, axis=0, keepdims=True)
         mixed_ref[t] = total.astype(jnp.bfloat16)
         return carry
 
@@ -81,9 +83,9 @@
 
 def gather_sum_kernel(top, pos_ref, back_ref, out_ref):
     def body(t, carry):
-        total = back_ref[pos_ref[top * t]].astype(jnp.float32)
+        total = back_ref[pos_ref[0, t]].astype(jnp.float32)
         for k in range(1, top):
-            total = total + back_ref[pos_ref[top * t + k]].astype(jnp.float32)
+            total = total + back_ref[pos_ref[k, t]].astype(jnp.float32)
         out_ref[t] = total.astype(jnp.bfloat16)
         return carry
 
@@ -122,19 +124,18 @@
     params = pltpu.CompilerParams(vmem_limit_bytes=32 << 20)
     call = functools.partial(pl.pallas_call, compiler_params=params, interpret=INTERPRET)
 
-    flat_ids = expert_ids.reshape(-1)
-    gates = gate_probs.astype(f32).reshape(-1)
+    gates = gate_probs.T.astype(f32)
     token_tiles = to_wire(tokens, sub)
     cot_tiles = to_wire(cotangent, sub)
 
     token_send, position = call(
         functools.partial(route_kernel, top, capacity),
-        out_shape=(wire_shape, jax.ShapeDtypeStruct((rows * top,), jnp.int32)),
+        out_shape=(wire_shape, jax.ShapeDtypeStruct((top, rows), jnp.int32)),
         in_specs=[smem(), vmem()],
         out_specs=(vmem(), smem()),
         scratch_shapes=[pltpu.SMEM((all_experts,), jnp.int32)],
         name="route",
-    )(flat_ids, token_tiles)
+    )(expert_ids.T, token_tiles)
     token_recv = exchange(token_send)
 
     routed_send = call(
@@ -146,44 +147,72 @@
     )(position, gates, cot_tiles)
     routed_recv = exchange(routed_send)
 
-    full_gate = lax.all_gather(w_gate[0], "dp", axis=0, tiled=True)
-    full_up = lax.all_gather(w_up[0], "dp", axis=0, tiled=True)
-    full_down = lax.all_gather(w_down[0], "dp", axis=1, tiled=True)
+    replicas = lax.axis_size("dp")
+    here = lax.axis_index("dp")
+
+    def to_replica(x, step):
+        return lax.ppermute(x, "dp", [(i, (i + step) % replicas) for i in range(replicas)])
+
+    def gather_replicas(shard, axis):
+        size = shard.shape[axis]
+        shape = list(shard.shape)
+        shape[axis] = size * replicas
+        full = jnp.zeros(shape, shard.dtype)
+        for step in range(replicas):
+            piece = to_replica(shard, step) if step else shard
+            place = (here - step) % replicas * size
+            full = lax.dynamic_update_slice_in_dim(full, piece, place, axis)
+        return full
+
+    def sum_replicas(part, axis):
+        size = part.shape[axis] // replicas
+        total = None
+        for step in range(replicas):
+            place = (here + step) % replicas * size
+            piece = lax.dynamic_slice_in_dim(part, place, size, axis)
+            piece = to_replica(piece, step) if step else piece
+            piece = piece.astype(f32)
+            total = piece if total is None else total + piece
+        return total
+
+    hid = w_gate.shape[2]
+    full_in = gather_replicas(jnp.concatenate([w_gate[0], w_up[0]], axis=1), 0)
+    full_down = gather_replicas(w_down[0], 1)
 
     def dot(a, b, dims):
         return lax.dot_general(a, b, (dims, ((), ())), preferred_element_type=f32)
 
     rows_in = to_rows(token_recv, width)
-    pre_gate = dot(rows_in, full_gate, ((1,), (0,)))
-    pre_up = dot(rows_in, full_up, ((1,), (0,)))
+    pre = dot(rows_in, full_in, ((1,), (0,)))
+    pre_gate, pre_up = pre[:, :hid], pre[:, hid:]
     activated, _ = silu_parts(pre_gate)
     hidden = (activated * pre_up).astype(bf16)
     expert_out = dot(hidden, full_down, ((1,), (0,))).astype(bf16)
     out_send = to_wire(expert_out, sub)
     back_out = exchange(out_send)
 
-    routed_recv, pre_gate, pre_up, _ = lax.optimization_barrier(
-        (routed_recv, pre_gate, pre_up, out_send)
-    )
+    routed_recv, pre, _ = lax.optimization_barrier((routed_recv, pre, out_send))
+    pre_gate, pre_up = pre[:, :hid], pre[:, hid:]
     activated, slope = silu_parts(pre_gate)
     routed_in = to_rows(routed_recv, width)
     grad_hidden = dot(routed_in, full_down, ((1,), (1,)))
-    grad_pre_gate = (grad_hidden * pre_up * slope).astype(bf16)
-    grad_pre_up = (grad_hidden * activated).astype(bf16)
-    pair_grad = dot(grad_pre_gate, full_gate, ((1,), (1,)))
-    pair_grad = (pair_grad + dot(grad_pre_up, full_up, ((1,), (1,)))).astype(bf16)
+    grad_pre = jnp.concatenate(
+        [
+            (grad_hidden * pre_up * slope).astype(bf16),
+            (grad_hidden * activated).astype(bf16),
+        ],
+        axis=1,
+    )
+    pair_grad = dot(grad_pre, full_in, ((1,), (1,))).astype(bf16)
     grad_send = to_wire(pair_grad, sub)
     back_grad = exchange(grad_send)
 
     def weight_part(a, b):
         return dot(a, b, ((0,), (0,))).astype(bf16)
 
-    def reduce_weight(part, axis):
-        return lax.psum_scatter(part, "dp", scatter_dimension=axis, tiled=True).astype(f32)[None]
-
-    grad_down_w = reduce_weight(weight_part(hidden, routed_in), 1)
-    grad_gate_w = reduce_weight(weight_part(rows_in, grad_pre_gate), 0)
-    grad_up_w = reduce_weight(weight_part(rows_in, grad_pre_up), 0)
+    grad_down_w = sum_replicas(weight_part(hidden, routed_in), 1)[None]
+    grad_in = sum_replicas(weight_part(rows_in, grad_pre), 0)
+    grad_gate_w, grad_up_w = grad_in[None, :, :hid], grad_in[None, :, hid:]
 
     mixed, dots = call(
         functools.partial(mix_kernel, top),
@@ -192,7 +221,7 @@
         out_specs=(vmem(), vmem()),
         name="mix",
     )(position, gates, cot_tiles, back_out)
-    grad_gates = jnp.sum(dots, axis=1).reshape(rows, top)
+    grad_gates = jnp.sum(dots, axis=1).reshape(top, rows).T
 
     grad_tokens = call(
         functools.partial(gather_sum_kernel, top),

time: 318 us -> 375 us (1.18)
  waiting for transfers between devices: 192 us -> 235 us
  starting transfers between devices: 30.9 us -> 53.6 us
  local copies, waits for them, and re-layouts: 18.6 us -> 35.1 us
  between operations: 14.3 us -> 1.02 us
  matrix products: 39.5 us -> 26.9 us
    ppermute x0 -> x12, waiting for transfers between devices: none -> 127 us  [to_replica(): lax.ppermute(x, 'dp', [(i, (i + step) % replicas) for i in range(replicas)])]
    all_to_all x4, waiting for transfers between devices: 160 us -> 108 us  [exchange(): lax.all_to_all(chunks, 'expert', 0, 0, tiled=True)]
    reduce_scatter x3 -> x0, waiting for transfers between devices: 29.2 us -> none  [reduce_weight(): lax.psum_scatter(part, 'dp', scatter_dimension=axis, tiled=True).astype(f32)]
    ppermute x0 -> x12, starting transfers between devices: none -> 17.3 us  [to_replica(): lax.ppermute(x, 'dp', [(i, (i + step) % replicas) for i in range(replicas)])]
    dot_general x9 -> x6, matrix products: 39.5 us -> 26.9 us  [dot(): return lax.dot_general(a, b, (dims, ((), ())), preferred_element_type=f32)]
    dynamic_update_slice x0 -> x7, local copies, waits for them, and re-layouts: none -> 12 us  [gather_replicas(): full = lax.dynamic_update_slice_in_dim(full, piece, place, axis)]
    all_to_all x4, starting transfers between devices: 30.5 us -> 36.3 us  [exchange(): lax.all_to_all(chunks, 'expert', 0, 0, tiled=True)]
    broadcast_in_dim x3 -> x1, other arithmetic: 6.43 us -> 1.27 us  [on_device(): grad_down_w = sum_replicas(weight_part(hidden, routed_in), 1)[None]]
  transfers between devices with their start and end apart: 10 -> 16, of which waited for: 5 -> 8; matrix products, arithmetic and copies ran while one was open for 19% -> 13% of each run, Pallas kernels for 2% -> 2%
where the time goes in v2:
time: 375 us; the launch traced here: 374 us
  waiting for transfers between devices  235 us (63%)
  starting transfers between devices  53.6 us (14%)
  local copies, waits for them, and re-layouts  35.1 us (9%)
  matrix products  26.9 us (7%)
  Pallas kernels  16.1 us (4%)
  other arithmetic  6.66 us (2%)
    ppermute x12, waiting for transfers between devices, to_replica(): lax.ppermute(x, 'dp', [(i, (i + step) % replicas) for i in range(replicas)])  127 us
    all_to_all x4, waiting for transfers between devices, exchange(): lax.all_to_all(chunks, 'expert', 0, 0, tiled=True)  108 us
    all_to_all x4, starting transfers between devices, exchange(): lax.all_to_all(chunks, 'expert', 0, 0, tiled=True)  36.3 us
    dot_general x6, matrix products, dot(): return lax.dot_general(a, b, (dims, ((), ())), preferred_element_type=f32)  26.9 us
    ppermute x12, starting transfers between devices, to_replica(): lax.ppermute(x, 'dp', [(i, (i + step) % replicas) for i in range(replicas)])  17.3 us
    dynamic_update_slice x7, local copies, waits for them, and re-layouts, gather_replicas(): full = lax.dynamic_update_slice_in_dim(full, piece, place, axis)  12 us
    another operation x2, local copies, waits for them, and re-layouts, exchange(): chunks = x.reshape(group, capacity * sub, LANES)  8.42 us
  transfers between devices with their start and end apart: 16, of which 8 were waited for; matrix products, arithmetic and copies ran while one was open for 13% of the time, Pallas kernels for 2%

profile of v2, /device:TPU:1, one launch (start us, length us, event | category | flops | bytes accessed | tf_op | source)
XLA Modules:
  0.0 374.1 jit_solution(9022009011057981442)
XLA Ops:
  2.5 5.5 %route.1 = (bf16[640,16,128]{2,1,0:T(8,128)(2,1)}, s32[4,128]{1,0:T(4,128)S(1)}) custom-call(s32[4,128]{1,0:T(4,128)S(1)} %bitcast.53, bf16[128,16,128]{2,1,0:T(8,128)(2,1)S(1)} %bitcast.50), custom_call_target="tpu_custom_call" | custom-call | tf_op jit(solution)/shard_map/route/pallas_call | solution.py:131
  8.0 13.0 %all-to-all-start = ((bf16[64,160,128]{2,1,0:T(8,128)(2,1)}), bf16[64,160,128]{2,1,0:T(8,128)(2,1)S(1)}, u32[]{:S(2)}, u32[]{:S(2)}) async-start(bf16[64,160,128]{2,1,0:T(8,128)(2,1)} %bitcast.2), calls=%async_computation | async-start | bytes 5242880 | tf_op jit(solution)/shard_map/all_to_all | solution.py:120
  22.1 4.1 %weigh.1 = bf16[640,16,128]{2,1,0:T(8,128)(2,1)} custom-call(s32[4,128]{1,0:T(4,128)S(1)} %get-tuple-element.12.pos_ref, f32[4,128]{1,0:T(4,128)S(1)} %convert_bitcast_fusion.gate_ref, bf16[128,16,128]{2,1,0:T(8,128)(2,1)S(1)} %bitcast.48), custom_call_target="tpu_custom_call" | custom-call | tf_op jit(solution)/shard_map/weigh/pallas_call | solution.py:141
  26.2 57.0 %all-to-all-done = bf16[64,160,128]{2,1,0:T(8,128)(2,1)S(1)} async-done(((bf16[64,160,128]{2,1,0:T(8,128)(2,1)}), bf16[64,160,128]{2,1,0:T(8,128)(2,1)S(1)}, u32[]{:S(2)}, u32[]{:S(2)}) %all-to-all-start) | async-done | bytes 2621472 | tf_op jit(solution)/shard_map/all_to_all | solution.py:120
  83.2 5.9 %all-to-all-start.2 = ((bf16[64,160,128]{2,1,0:T(8,128)(2,1)}), bf16[64,160,128]{2,1,0:T(8,128)(2,1)}, u32[]{:S(2)}, u32[]{:S(2)}) async-start(bf16[64,160,128]{2,1,0:T(8,128)(2,1)} %bitcast.7), calls=%async_computation.2 | async-start | bytes 5242880 | tf_op jit(solution)/shard_map/all_to_all | solution.py:120
  90.5 2.5 broadcast_in_dim.15
  100.2 3.6 collective-permute-done.3
  107.7 53.4 %collective-permute-done.4 = bf16[512,512]{1,0:T(8,128)(2,1)} collective-permute-done((bf16[512,512]{1,0:T(8,128)(2,1)}, bf16[512,512]{1,0:T(8,128)(2,1)}, u32[]{:S(2)}, u32[]{:S(2)}) %collective-permute-start.4) | collective-permute-done | bytes 524320 | tf_op jit(solution)/shard_map/ppermute | solution.py:154
  162.2 3.5 collective-permute-done.5
  166.8 3.1 constant_dynamic-update-slice_fusion.6
  169.9 2.3 constant_dynamic-update-slice_fusion.5
  172.2 2.3 constant_dynamic-update-slice_fusion.4
  174.4 3.1 reshape_reshape.9
  177.5 5.4 %fusion.8 = f32[640,1024]{1,0:T(8,128)S(1)} fusion(bf16[640,2048]{1,0:T(8,128)(2,1)} %reshape_reshape.9, bf16[2048,1024]{1,0:T(8,128)(2,1)} %constant_dynamic-update-slice_fusion.4), kind=kOutput, calls=%fused_computation.39 | convolution fusion | flops 2684354560 | bytes 9437184 | tf_op jit(solution)/shard_map/dot_general | solution.py:183
  182.9 5.3 %multiply_convert_fusion.1 = (bf16[640,512]{1,0:T(8,128)(2,1)S(1)}, bf16[640,512]{1,0:T(8,128)(2,1)S(1)}) fusion(f32[640,1024]{1,0:T(8,128)S(1)} %fusion.8, bf16[512,2048]{1,0:T(8,128)(2,1)} %copy-done.5, bf16[80,8,16,128]{3,2,1,0:T(8,128)(2,1)} %bitcast.22), kind=kOutput, calls=%fused_computation.14 | convolution fusion | flops 1346437120 | bytes 8650752 | tf_op jit(solution)/shard_map/dot_general | solution.py:183
  189.3 5.3 %convolution_convert_fusion.2 = bf16[640,2048]{1,0:T(8,128)(2,1)S(1)} fusion(bf16[2048,1024]{1,0:T(8,128)(2,1)} %constant_dynamic-update-slice_fusion.4, bf16[640,512]{1,0:T(8,128)(2,1)S(1)} %get-tuple-element.22, bf16[640,512]{1,0:T(8,128)(2,1)S(1)} %get-tuple-element.21), kind=kOutput, calls=%fused_computation.2 | convolution fusion | flops 2688286720 | bytes 8126464 | tf_op jit(solution)/shard_map/dot_general | solution.py:183
  194.7 3.2 reshape_reshape.11
  197.8 11.5 %all-to-all-start.3 = ((bf16[64,160,128]{2,1,0:T(8,128)(2,1)}), bf16[64,160,128]{2,1,0:T(8,128)(2,1)S(1)}, u32[]{:S(2)}, u32[]{:S(2)}) async-start(bf16[64,160,128]{2,1,0:T(8,128)(2,1)} %reshape_reshape.11), calls=%async_computation.3 | async-start | bytes 5242880 | tf_op jit(solution)/shard_map/all_to_all | solution.py:120
  209.3 2.2 fusion.5
  212.4 3.0 convolution_convert_fusion.1
  215.5 5.3 %reshape_reshape.10 = bf16[64,160,128]{2,1,0:T(8,128)(2,1)} reshape(bf16[640,2048]{1,0:T(8,128)(2,1)} %convolution_convert_fusion.1) | data formatting | bytes 5242880 | tf_op jit(solution)/shard_map/reshape;reshape | solution.py:119
  220.7 50.8 %all-to-all-done.3 = bf16[64,160,128]{2,1,0:T(8,128)(2,1)S(1)} async-done(((bf16[64,160,128]{2,1,0:T(8,128)(2,1)}), bf16[64,160,128]{2,1,0:T(8,128)(2,1)S(1)}, u32[]{:S(2)}, u32[]{:S(2)}) %all-to-all-start.3) | async-done | bytes 2621472 | tf_op jit(solution)/shard_map/all_to_all | solution.py:120
  271.6 5.9 %all-to-all-start.1 = ((bf16[64,160,128]{2,1,0:T(8,128)(2,1)}), bf16[64,160,128]{2,1,0:T(8,128)(2,1)}, u32[]{:S(2)}, u32[]{:S(2)}) async-start(bf16[64,160,128]{2,1,0:T(8,128)(2,1)} %reshape_reshape.10), calls=%async_computation.1 | async-start | bytes 5242880 | tf_op jit(solution)/shard_map/all_to_all | solution.py:120
  277.5 3.9 %convolution_convert_fusion.3 = bf16[512,2048]{1,0:T(8,128)(2,1)S(1)} fusion(bf16[640,512]{1,0:T(8,128)(2,1)} %copy-done.7, bf16[80,8,16,128]{3,2,1,0:T(8,128)(2,1)} %bitcast.22), kind=kOutput, calls=%fused_computation.3 | convolution fusion | flops 1343225856 | bytes 5373952 | tf_op jit(solution)/shard_map/dot_general | solution.py:183
  281.6 2.6 collective-permute-start.11
  284.2 3.9 %convolution_convert_fusion = bf16[2048,1024]{1,0:T(8,128)(2,1)S(1)} fusion(bf16[640,2048]{1,0:T(8,128)(2,1)S(1)} %copy-done.3, bf16[640,512]{1,0:T(8,128)(2,1)S(1)} %copy-done.14, bf16[640,512]{1,0:T(8,128)(2,1)S(1)} %copy-done.12), kind=kOutput, calls=%fused_computation | convolution fusion | flops 2689073152 | bytes 8126464 | tf_op jit(solution)/shard_map/dot_general | solution.py:183
  291.2 2.4 collective-permute-start.10
  293.6 2.2 collective-permute-done.11
  297.0 52.0 %collective-permute-done.10 = bf16[512,512]{1,0:T(8,128)(2,1)S(1)} collective-permute-done((bf16[512,512]{1,0:T(8,128)(2,1)S(1)}, bf16[512,512]{1,0:T(8,128)(2,1)S(1)}, u32[]{:S(2)}, u32[]{:S(2)}) %collective-permute-start.10) | collective-permute-done | bytes 524320 | tf_op jit(solution)/shard_map/ppermute | solution.py:154
  349.0 12.3 %collective-permute-done.9 = bf16[512,512]{1,0:T(8,128)(2,1)S(1)} collective-permute-done((bf16[512,512]{1,0:T(8,128)(2,1)S(1)}, bf16[512,512]{1,0:T(8,128)(2,1)S(1)}, u32[]{:S(2)}, u32[]{:S(2)}) %collective-permute-start.9) | collective-permute-done | bytes 524320 | tf_op jit(solution)/shard_map/ppermute | solution.py:154
  364.9 2.1 gather_sum.1
  367.8 4.4 %mix.1 = (bf16[128,16,128]{2,1,0:T(8,128)(2,1)S(1)}, f32[512,128]{1,0:T(8,128)S(1)}) custom-call(s32[4,128]{1,0:T(4,128)S(1)} %get-tuple-element.12.pos_ref, f32[4,128]{1,0:T(4,128)S(1)} %convert_bitcast_fusion.gate_ref, bf16[128,16,128]{2,1,0:T(8,128)(2,1)S(1)} %bitcast.49, bf16[640,16,128]{2,1,0:T(8,128)(2,1)} %bitcast.6.back_ref), custom_call_target="tpu_custom_call" | custom-call | tf_op jit(solution)/shard_map/mix/pallas_call | solution.py:217
  (64 shorter events, 30.3 us)
Async XLA Ops:
  1.8 0.7 copy-start.2
  8.0 14.2 %copy-start.10 = (bf16[128,4]{0,1:T(4,128)(2,1)S(1)}, bf16[128,4]{0,1:T(4,128)(2,1)}, u32[]{:S(2)}) copy-start(bf16[128,4]{0,1:T(4,128)(2,1)} %param.10) | copy-start | bytes 3076
  8.0 75.2 %all-to-all-start = ((bf16[64,160,128]{2,1,0:T(8,128)(2,1)}), bf16[64,160,128]{2,1,0:T(8,128)(2,1)S(1)}, u32[]{:S(2)}, u32[]{:S(2)}) async-start(bf16[64,160,128]{2,1,0:T(8,128)(2,1)} %bitcast.2), calls=%async_computation | async-start | bytes 5242880 | tf_op jit(solution)/shard_map/all_to_all | solution.py:120
  83.2 99.7 %all-to-all-start.2 = ((bf16[64,160,128]{2,1,0:T(8,128)(2,1)}), bf16[64,160,128]{2,1,0:T(8,128)(2,1)}, u32[]{:S(2)}, u32[]{:S(2)}) async-start(bf16[64,160,128]{2,1,0:T(8,128)(2,1)} %bitcast.7), calls=%async_computation.2 | async-start | bytes 5242880 | tf_op jit(solution)/shard_map/all_to_all | solution.py:120
  89.1 14.7 %collective-permute-start.3 = (bf16[512,512]{1,0:T(8,128)(2,1)}, bf16[512,512]{1,0:T(8,128)(2,1)}, u32[]{:S(2)}, u32[]{:S(2)}) collective-permute-start(bf16[512,512]{1,0:T(8,128)(2,1)} %bitcast.5), channel_id=1, source_target_pairs={{0,64},{64,128},{128,192},{192,0},{1,65},{65,129},{129,193},{193,1... | collective-permute-start | bytes 1572872 | tf_op jit(solution)/shard_map/ppermute | solution.py:154
  90.5 2.5 copy-start.8
  90.5 2.5 copy-start.9
  94.6 72.2 %collective-permute-start = (bf16[512,1024]{1,0:T(8,128)(2,1)}, bf16[512,1024]{1,0:T(8,128)(2,1)}, u32[]{:S(2)}, u32[]{:S(2)}) collective-permute-start(bf16[512,1024]{1,0:T(8,128)(2,1)} %get-tuple-element.28), channel_id=1, source_target_pairs={{0,64},{64,128},{128,192},{192,0},{1,65},{65,129},{129,193},{193,1... | collective-permute-start | bytes 3145736 | tf_op jit(solution)/shard_map/ppermute | solution.py:154
  95.9 74.0 %collective-permute-start.1 = (bf16[512,1024]{1,0:T(8,128)(2,1)}, bf16[512,1024]{1,0:T(8,128)(2,1)}, u32[]{:S(2)}, u32[]{:S(2)}) collective-permute-start(bf16[512,1024]{1,0:T(8,128)(2,1)} %get-tuple-element.28), channel_id=1, source_target_pairs={{0,128},{64,192},{128,0},{192,64},{1,129},{65,193},{129,1},{193,65... | collective-permute-start | bytes 3145736 | tf_op jit(solution)/shard_map/ppermute | solution.py:154
  97.3 63.8 %collective-permute-start.4 = (bf16[512,512]{1,0:T(8,128)(2,1)}, bf16[512,512]{1,0:T(8,128)(2,1)}, u32[]{:S(2)}, u32[]{:S(2)}) collective-permute-start(bf16[512,512]{1,0:T(8,128)(2,1)} %bitcast.5), channel_id=1, source_target_pairs={{0,128},{64,192},{128,0},{192,64},{1,129},{65,193},{129,1},{193,65... | collective-permute-start | bytes 1572872 | tf_op jit(solution)/shard_map/ppermute | solution.py:154
  98.9 73.3 %collective-permute-start.2 = (bf16[512,1024]{1,0:T(8,128)(2,1)}, bf16[512,1024]{1,0:T(8,128)(2,1)}, u32[]{:S(2)}, u32[]{:S(2)}) collective-permute-start(bf16[512,1024]{1,0:T(8,128)(2,1)} %get-tuple-element.28), channel_id=1, source_target_pairs={{0,192},{64,0},{128,64},{192,128},{1,193},{65,1},{129,65},{193,129... | collective-permute-start | bytes 3145736 | tf_op jit(solution)/shard_map/ppermute | solution.py:154
  103.8 61.9 %collective-permute-start.5 = (bf16[512,512]{1,0:T(8,128)(2,1)}, bf16[512,512]{1,0:T(8,128)(2,1)}, u32[]{:S(2)}, u32[]{:S(2)}) collective-permute-start(bf16[512,512]{1,0:T(8,128)(2,1)} %bitcast.5), channel_id=1, source_target_pairs={{0,192},{64,0},{128,64},{192,128},{1,193},{65,1},{129,65},{193,129... | collective-permute-start | bytes 1572872 | tf_op jit(solution)/shard_map/ppermute | solution.py:154
  166.8 5.4 %copy-start.5 = (bf16[512,2048]{1,0:T(8,128)(2,1)}, bf16[512,2048]{1,0:T(8,128)(2,1)S(1)}, u32[]{:S(2)}) copy-start(bf16[512,2048]{1,0:T(8,128)(2,1)S(1)} %constant_dynamic-update-slice_fusion) | copy-start | bytes 6291460
  182.9 5.4 %copy-start.4 = (f32[640,1024]{1,0:T(8,128)}, f32[640,1024]{1,0:T(8,128)S(1)}, u32[]{:S(2)}) copy-start(f32[640,1024]{1,0:T(8,128)S(1)} %fusion.8) | copy-start | bytes 7864324
  188.3 0.8 copy-start.11
  188.3 1.0 copy-start.13
  197.8 73.7 %all-to-all-start.3 = ((bf16[64,160,128]{2,1,0:T(8,128)(2,1)}), bf16[64,160,128]{2,1,0:T(8,128)(2,1)S(1)}, u32[]{:S(2)}, u32[]{:S(2)}) async-start(bf16[64,160,128]{2,1,0:T(8,128)(2,1)} %reshape_reshape.11), calls=%async_computation.3 | async-start | bytes 5242880 | tf_op jit(solution)/shard_map/all_to_all | solution.py:120
  209.3 3.1 copy-start.6
  211.6 0.8 copy-start.7
  271.6 96.2 %all-to-all-start.1 = ((bf16[64,160,128]{2,1,0:T(8,128)(2,1)}), bf16[64,160,128]{2,1,0:T(8,128)(2,1)}, u32[]{:S(2)}, u32[]{:S(2)}) async-start(bf16[64,160,128]{2,1,0:T(8,128)(2,1)} %reshape_reshape.10), calls=%async_computation.1 | async-start | bytes 5242880 | tf_op jit(solution)/shard_map/all_to_all | solution.py:120
  277.5 6.7 %copy-start.12 = (bf16[640,512]{1,0:T(8,128)(2,1)S(1)}, bf16[640,512]{1,0:T(8,128)(2,1)}, u32[]{:S(2)}) copy-start(bf16[640,512]{1,0:T(8,128)(2,1)} %copy-done.11) | copy-start | bytes 1966084
  277.5 6.7 %copy-start.14 = (bf16[640,512]{1,0:T(8,128)(2,1)S(1)}, bf16[640,512]{1,0:T(8,128)(2,1)}, u32[]{:S(2)}) copy-start(bf16[640,512]{1,0:T(8,128)(2,1)} %copy-done.13) | copy-start | bytes 1966084
  281.4 2.8 copy-start.3
  281.6 14.2 %collective-permute-start.11 = (bf16[512,512]{1,0:T(8,128)(2,1)S(1)}, bf16[512,512]{1,0:T(8,128)(2,1)S(1)}, u32[]{:S(2)}, u32[]{:S(2)}) collective-permute-start(bf16[512,512]{1,0:T(8,128)(2,1)S(1)} %get-tuple-element.24), channel_id=1, source_target_pairs={{0,192},{64,0},{128,64},{192,128},{1,193},{65,1},{129,65},{193,129... | collective-permute-start | bytes 1572872 | tf_op jit(solution)/shard_map/ppermute | solution.py:154
  288.4 74.1 %collective-permute-start.8 = (bf16[512,1024]{1,0:T(8,128)(2,1)S(1)}, bf16[512,1024]{1,0:T(8,128)(2,1)S(1)}, u32[]{:S(2)}, u32[]{:S(2)}) collective-permute-start(bf16[512,1024]{1,0:T(8,128)(2,1)S(1)} %get-tuple-element.19), channel_id=1, source_target_pairs={{0,192},{64,0},{128,64},{192,128},{1,193},{65,1},{129,65},{193,129... | collective-permute-start | bytes 3145736 | tf_op jit(solution)/shard_map/ppermute | solution.py:154
  289.7 72.8 %collective-permute-start.7 = (bf16[512,1024]{1,0:T(8,128)(2,1)S(1)}, bf16[512,1024]{1,0:T(8,128)(2,1)S(1)}, u32[]{:S(2)}, u32[]{:S(2)}) collective-permute-start(bf16[512,1024]{1,0:T(8,128)(2,1)S(1)} %get-tuple-element.20), channel_id=1, source_target_pairs={{0,128},{64,192},{128,0},{192,64},{1,129},{65,193},{129,1},{193,65... | collective-permute-start | bytes 3145736 | tf_op jit(solution)/shard_map/ppermute | solution.py:154
  291.2 71.4 %collective-permute-start.6 = (bf16[512,1024]{1,0:T(8,128)(2,1)S(1)}, bf16[512,1024]{1,0:T(8,128)(2,1)S(1)}, u32[]{:S(2)}, u32[]{:S(2)}) collective-permute-start(bf16[512,1024]{1,0:T(8,128)(2,1)S(1)} %get-tuple-element.18), channel_id=1, source_target_pairs={{0,64},{64,128},{128,192},{192,0},{1,65},{65,129},{129,193},{193,1... | collective-permute-start | bytes 3145736 | tf_op jit(solution)/shard_map/ppermute | solution.py:154
  291.2 57.8 %collective-permute-start.10 = (bf16[512,512]{1,0:T(8,128)(2,1)S(1)}, bf16[512,512]{1,0:T(8,128)(2,1)S(1)}, u32[]{:S(2)}, u32[]{:S(2)}) collective-permute-start(bf16[512,512]{1,0:T(8,128)(2,1)S(1)} %get-tuple-element.25), channel_id=1, source_target_pairs={{0,128},{64,192},{128,0},{192,64},{1,129},{65,193},{129,1},{193,65... | collective-permute-start | bytes 1572872 | tf_op jit(solution)/shard_map/ppermute | solution.py:154
  295.8 65.5 %collective-permute-start.9 = (bf16[512,512]{1,0:T(8,128)(2,1)S(1)}, bf16[512,512]{1,0:T(8,128)(2,1)S(1)}, u32[]{:S(2)}, u32[]{:S(2)}) collective-permute-start(bf16[512,512]{1,0:T(8,128)(2,1)S(1)} %get-tuple-element.23), channel_id=1, source_target_pairs={{0,64},{64,128},{128,192},{192,0},{1,65},{65,129},{129,193},{193,1... | collective-permute-start | bytes 1572872 | tf_op jit(solution)/shard_map/ppermute | solution.py:154
  367.0 0.8 copy-start
  367.8 4.4 %copy-start.1 = (bf16[128,16,128]{2,1,0:T(8,128)(2,1)S(1)}, bf16[128,16,128]{2,1,0:T(8,128)(2,1)}, u32[]{:S(2)}) copy-start(bf16[128,16,128]{2,1,0:T(8,128)(2,1)} %copy-done) | copy-start | bytes 1572868

commit v3 on v2

--- a/solution.py
+++ b/solution.py
@@ -31,26 +31,40 @@
     lax.fori_loop(0, rows // step, body, 0)
 
 
-def route_kernel(top, capacity, ids_ref, tok_ref, out_ref, pos_ref, count_ref):
-    def reset(i, carry):
-        count_ref[i] = 0
-        return carry
-
-    lax.fori_loop(0, count_ref.shape[0], reset, 0)
+def for_each(count, body, unroll=4):
+    def step(i, carry):
+        for j in range(unroll):
+            body(unroll * i + j)
+        return carry
+
+    lax.fori_loop(0, count // unroll, step, 0)
+
+
+def route_kernel(capacity, experts, ids_ref, tok_ref, out_ref, pos_ref, place_ref, sem):
+    top, rows = ids_ref.shape
+    f32 = jnp.float32
+    expert = lax.broadcasted_iota(jnp.int32, (experts, rows), 0)
+    hits = [ids_ref[pl.ds(k, 1), :] == expert for k in range(top)]
+    named = sum(hit.astype(f32) for hit in hits).astype(jnp.bfloat16)
+    first = lax.broadcasted_iota(jnp.int32, (rows, rows), 0)
+    second = lax.broadcasted_iota(jnp.int32, (rows, rows), 1)
+    before = (first < second).astype(f32).astype(jnp.bfloat16)
+    rank = jnp.dot(named, before, preferred_element_type=f32)
+    slot = (expert * capacity).astype(f32) + rank
+    for k in range(top):
+        chosen = jnp.sum(jnp.where(hits[k], slot, 0.0), axis=0, keepdims=True)
+        pos_ref[pl.ds(k, 1), :] = chosen.astype(jnp.int32)
+    copy = pltpu.make_async_copy(pos_ref, place_ref, sem)
+    copy.start()
     clear_rows(out_ref)
-
-    def body(t, carry):
+    copy.wait()
+
+    def body(t):
         row = tok_ref[t]
-        names = [ids_ref[k, t] for k in range(top)]
-        slots = [count_ref[e] for e in names]
         for k in range(top):
-            count_ref[names[k]] = slots[k] + 1
-            place = names[k] * capacity + slots[k]
-            pos_ref[k, t] = place
-            out_ref[place] = row
-        return carry
-
-    lax.fori_loop(0, tok_ref.shape[0], body, 0)
+            out_ref[place_ref[k, t]] = row
+
+    for_each(rows, body)
 
 
 def weigh_kernel(top, pos_ref, gate_ref, cot_ref, out_ref):
@@ -82,14 +96,13 @@
 
 
 def gather_sum_kernel(top, pos_ref, back_ref, out_ref):
-    def body(t, carry):
+    def body(t):
         total = back_ref[pos_ref[0, t]].astype(jnp.float32)
         for k in range(1, top):
             total = total + back_ref[pos_ref[k, t]].astype(jnp.float32)
         out_ref[t] = total.astype(jnp.bfloat16)
-        return carry
-
-    lax.fori_loop(0, out_ref.shape[0], body, 0)
+
+    for_each(out_ref.shape[0], body, 8)
 
 
 def silu_parts(pre_gate):
@@ -129,11 +142,11 @@
     cot_tiles = to_wire(cotangent, sub)
 
     token_send, position = call(
-        functools.partial(route_kernel, top, capacity),
+        functools.partial(route_kernel, capacity, all_experts),
         out_shape=(wire_shape, jax.ShapeDtypeStruct((top, rows), jnp.int32)),
-        in_specs=[smem(), vmem()],
-        out_specs=(vmem(), smem()),
-        scratch_shapes=[pltpu.SMEM((all_experts,), jnp.int32)],
+        in_specs=[vmem(), vmem()],
+        out_specs=(vmem(), vmem()),
+        scratch_shapes=[pltpu.SMEM((top, rows), jnp.int32), pltpu.SemaphoreType.DMA],
         name="route",
     )(expert_ids.T, token_tiles)
     token_recv = exchange(token_send)
@@ -223,6 +236,7 @@
     )(position, gates, cot_tiles, back_out)
     grad_gates = jnp.sum(dots, axis=1).reshape(top, rows).T
 
+    mixed, back_grad = lax.optimization_barrier((to_rows(mixed, width), back_grad))
     grad_tokens = call(
         functools.partial(gather_sum_kernel, top),
         out_shape=token_shape,
@@ -231,7 +245,7 @@
         name="gather_sum",
     )(position, back_grad)
     return (
-        to_rows(mixed, width),
+        mixed,
         to_rows(grad_tokens, width),
         grad_gates,
         grad_gate_w,

time: 375 us -> 365 us (0.973)
  waiting for transfers between devices: 235 us -> 229 us
    all_to_all x4, waiting for transfers between devices: 108 us -> 101 us  [exchange(): lax.all_to_all(chunks, 'expert', 0, 0, tiled=True)]
    unnamed x32 -> x30, local copies, waits for them, and re-layouts: 5.68 us -> 8.78 us
  transfers between devices with their start and end apart: 16 -> 16, of which waited for: 8 -> 8; matrix products, arithmetic and copies ran while one was open for 13% -> 17% of each run, Pallas kernels for 2% -> 2%
where the time goes in v3:
time: 365 us; the launch traced here: 364 us
  waiting for transfers between devices  229 us (63%)
  starting transfers between devices  53.4 us (15%)
  local copies, waits for them, and re-layouts  37 us (10%)
  matrix products  26.2 us (7%)
  Pallas kernels  13 us (4%)
  other arithmetic  4.8 us (1%)
    ppermute x12, waiting for transfers between devices, to_replica(): lax.ppermute(x, 'dp', [(i, (i + step) % replicas) for i in range(replicas)])  127 us
    all_to_all x4, waiting for transfers between devices, exchange(): lax.all_to_all(chunks, 'expert', 0, 0, tiled=True)  101 us
    all_to_all x4, starting transfers between devices, exchange(): lax.all_to_all(chunks, 'expert', 0, 0, tiled=True)  36.3 us
    dot_general x6, matrix products, dot(): return lax.dot_general(a, b, (dims, ((), ())), preferred_element_type=f32)  26.2 us
    ppermute x12, starting transfers between devices, to_replica(): lax.ppermute(x, 'dp', [(i, (i + step) % replicas) for i in range(replicas)])  17.1 us
    dynamic_update_slice x7, local copies, waits for them, and re-layouts, gather_replicas(): full = lax.dynamic_update_slice_in_dim(full, piece, place, axis)  12 us
    unnamed x30, local copies, waits for them, and re-layouts  8.78 us
    another operation x2, local copies, waits for them, and re-layouts, exchange(): chunks = x.reshape(group, capacity * sub, LANES)  8.41 us
  transfers between devices with their start and end apart: 16, of which 8 were waited for; matrix products, arithmetic and copies ran while one was open for 17% of the time, Pallas kernels for 2%

profile of v3, /device:TPU:1, one launch (start us, length us, event | category | flops | bytes accessed | tf_op | source)
XLA Modules:
  0.0 364.0 jit_solution(10618136639324825563)
XLA Ops:
  2.5 3.2 route.1
  5.7 13.0 %all-to-all-start = ((bf16[64,160,128]{2,1,0:T(8,128)(2,1)}), bf16[64,160,128]{2,1,0:T(8,128)(2,1)S(1)}, u32[]{:S(2)}, u32[]{:S(2)}) async-start(bf16[64,160,128]{2,1,0:T(8,128)(2,1)} %bitcast.2), calls=%async_computation | async-start | bytes 5242880 | tf_op jit(solution)/shard_map/all_to_all | solution.py:133
  19.8 4.1 %weigh.1 = bf16[640,16,128]{2,1,0:T(8,128)(2,1)} custom-call(s32[4,128]{1,0:T(4,128)S(1)} %get-tuple-element.14.pos_ref, f32[4,128]{1,0:T(4,128)S(1)} %convert_bitcast_fusion.gate_ref, bf16[128,16,128]{2,1,0:T(8,128)(2,1)S(1)} %bitcast.50), custom_call_target="tpu_custom_call" | custom-call | tf_op jit(solution)/shard_map/weigh/pallas_call | solution.py:154
  23.9 57.0 %all-to-all-done = bf16[64,160,128]{2,1,0:T(8,128)(2,1)S(1)} async-done(((bf16[64,160,128]{2,1,0:T(8,128)(2,1)}), bf16[64,160,128]{2,1,0:T(8,128)(2,1)S(1)}, u32[]{:S(2)}, u32[]{:S(2)}) %all-to-all-start) | async-done | bytes 2621472 | tf_op jit(solution)/shard_map/all_to_all | solution.py:133
  80.9 5.9 %all-to-all-start.2 = ((bf16[64,160,128]{2,1,0:T(8,128)(2,1)}), bf16[64,160,128]{2,1,0:T(8,128)(2,1)}, u32[]{:S(2)}, u32[]{:S(2)}) async-start(bf16[64,160,128]{2,1,0:T(8,128)(2,1)} %bitcast.7), calls=%async_computation.2 | async-start | bytes 5242880 | tf_op jit(solution)/shard_map/all_to_all | solution.py:133
  88.2 2.5 broadcast_in_dim.15
  90.7 1.6 pad_maximum_fusion.1
  95.0 1.6 collective-permute-start.4
  97.9 3.6 collective-permute-done.3
  105.4 53.4 %collective-permute-done.4 = bf16[512,512]{1,0:T(8,128)(2,1)} collective-permute-done((bf16[512,512]{1,0:T(8,128)(2,1)}, bf16[512,512]{1,0:T(8,128)(2,1)}, u32[]{:S(2)}, u32[]{:S(2)}) %collective-permute-start.4) | collective-permute-done | bytes 524320 | tf_op jit(solution)/shard_map/ppermute | solution.py:167
  159.9 3.5 collective-permute-done.5
  164.5 3.0 constant_dynamic-update-slice_fusion.6
  167.5 2.3 constant_dynamic-update-slice_fusion.5
  169.8 2.3 constant_dynamic-update-slice_fusion.4
  172.1 3.0 reshape_reshape.9
  175.1 5.4 %fusion.8 = f32[640,1024]{1,0:T(8,128)S(1)} fusion(bf16[640,2048]{1,0:T(8,128)(2,1)} %reshape_reshape.9, bf16[2048,1024]{1,0:T(8,128)(2,1)} %constant_dynamic-update-slice_fusion.4), kind=kOutput, calls=%fused_computation.39 | convolution fusion | flops 2684354560 | bytes 9437184 | tf_op jit(solution)/shard_map/dot_general | solution.py:196
  185.4 3.2 reshape_reshape.10
  188.6 11.5 %all-to-all-start.1 = ((bf16[64,160,128]{2,1,0:T(8,128)(2,1)}), bf16[64,160,128]{2,1,0:T(8,128)(2,1)S(1)}, u32[]{:S(2)}, u32[]{:S(2)}) async-start(bf16[64,160,128]{2,1,0:T(8,128)(2,1)} %reshape_reshape.10), calls=%async_computation.1 | async-start | bytes 5242880 | tf_op jit(solution)/shard_map/all_to_all | solution.py:133
  200.1 5.1 %multiply_convert_fusion.1 = (bf16[640,512]{1,0:T(8,128)(2,1)S(1)}, bf16[640,512]{1,0:T(8,128)(2,1)S(1)}) fusion(f32[640,1024]{1,0:T(8,128)} %copy-done.2, bf16[512,2048]{1,0:T(8,128)(2,1)} %copy-done.3, bf16[80,8,16,128]{3,2,1,0:T(8,128)(2,1)} %bitcast.22), kind=kOutput, calls=%fused_computation.14 | convolution fusion | flops 1346437120 | bytes 8650752 | tf_op jit(solution)/shard_map/dot_general | solution.py:196
  206.2 6.4 %convolution_convert_fusion.2 = bf16[640,2048]{1,0:T(8,128)(2,1)} fusion(bf16[2048,1024]{1,0:T(8,128)(2,1)} %constant_dynamic-update-slice_fusion.4, bf16[640,512]{1,0:T(8,128)(2,1)S(1)} %get-tuple-element.26, bf16[640,512]{1,0:T(8,128)(2,1)S(1)} %get-tuple-element.25), kind=kOutput, calls=%fused_computation.2 | convolution fusion | flops 2688286720 | bytes 8126464 | tf_op jit(solution)/shard_map/dot_general | solution.py:196
  212.6 5.2 %reshape_reshape.11 = bf16[64,160,128]{2,1,0:T(8,128)(2,1)} reshape(bf16[640,2048]{1,0:T(8,128)(2,1)} %convolution_convert_fusion.2) | data formatting | bytes 5242880 | tf_op jit(solution)/shard_map/reshape;reshape | solution.py:132
  217.8 44.5 %all-to-all-done.1 = bf16[64,160,128]{2,1,0:T(8,128)(2,1)S(1)} async-done(((bf16[64,160,128]{2,1,0:T(8,128)(2,1)}), bf16[64,160,128]{2,1,0:T(8,128)(2,1)S(1)}, u32[]{:S(2)}, u32[]{:S(2)}) %all-to-all-start.1) | async-done | bytes 2621472 | tf_op jit(solution)/shard_map/all_to_all | solution.py:133
  262.3 5.9 %all-to-all-start.3 = ((bf16[64,160,128]{2,1,0:T(8,128)(2,1)}), bf16[64,160,128]{2,1,0:T(8,128)(2,1)}, u32[]{:S(2)}, u32[]{:S(2)}) async-start(bf16[64,160,128]{2,1,0:T(8,128)(2,1)} %reshape_reshape.11), calls=%async_computation.3 | async-start | bytes 5242880 | tf_op jit(solution)/shard_map/all_to_all | solution.py:133
  268.3 3.9 %convolution_convert_fusion.3 = bf16[512,2048]{1,0:T(8,128)(2,1)S(1)} fusion(bf16[640,512]{1,0:T(8,128)(2,1)} %copy-done.5, bf16[80,8,16,128]{3,2,1,0:T(8,128)(2,1)} %bitcast.22), kind=kOutput, calls=%fused_computation.3 | convolution fusion | flops 1343225856 | bytes 5373952 | tf_op jit(solution)/shard_map/dot_general | solution.py:196
  272.4 2.4 collective-permute-start.11
  274.8 3.9 %convolution_convert_fusion = bf16[2048,1024]{1,0:T(8,128)(2,1)S(1)} fusion(bf16[640,2048]{1,0:T(8,128)(2,1)S(1)} %copy-done.1, bf16[640,512]{1,0:T(8,128)(2,1)S(1)} %copy-done.12, bf16[640,512]{1,0:T(8,128)(2,1)S(1)} %copy-done.10), kind=kOutput, calls=%fused_computation | convolution fusion | flops 2689073152 | bytes 8126464 | tf_op jit(solution)/shard_map/dot_general | solution.py:196
  282.0 2.1 collective-permute-start.10
  284.1 2.2 collective-permute-done.11
  287.5 52.2 %collective-permute-done.10 = bf16[512,512]{1,0:T(8,128)(2,1)S(1)} collective-permute-done((bf16[512,512]{1,0:T(8,128)(2,1)S(1)}, bf16[512,512]{1,0:T(8,128)(2,1)S(1)}, u32[]{:S(2)}, u32[]{:S(2)}) %collective-permute-start.10) | collective-permute-done | bytes 524320 | tf_op jit(solution)/shard_map/ppermute | solution.py:167
  339.7 12.3 %collective-permute-done.9 = bf16[512,512]{1,0:T(8,128)(2,1)S(1)} collective-permute-done((bf16[512,512]{1,0:T(8,128)(2,1)S(1)}, bf16[512,512]{1,0:T(8,128)(2,1)S(1)}, u32[]{:S(2)}, u32[]{:S(2)}) %collective-permute-start.9) | collective-permute-done | bytes 524320 | tf_op jit(solution)/shard_map/ppermute | solution.py:167
  355.6 3.2 mix.1
  359.7 2.6 gather_sum.1
  (61 shorter events, 31.2 us)
Async XLA Ops:
  1.8 0.7 copy-start
  5.7 14.2 %copy-start.8 = (bf16[128,4]{0,1:T(4,128)(2,1)S(1)}, bf16[128,4]{0,1:T(4,128)(2,1)}, u32[]{:S(2)}) copy-start(bf16[128,4]{0,1:T(4,128)(2,1)} %param.10) | copy-start | bytes 3076
  5.7 75.2 %all-to-all-start = ((bf16[64,160,128]{2,1,0:T(8,128)(2,1)}), bf16[64,160,128]{2,1,0:T(8,128)(2,1)S(1)}, u32[]{:S(2)}, u32[]{:S(2)}) async-start(bf16[64,160,128]{2,1,0:T(8,128)(2,1)} %bitcast.2), calls=%async_computation | async-start | bytes 5242880 | tf_op jit(solution)/shard_map/all_to_all | solution.py:133
  80.9 107.7 %all-to-all-start.2 = ((bf16[64,160,128]{2,1,0:T(8,128)(2,1)}), bf16[64,160,128]{2,1,0:T(8,128)(2,1)}, u32[]{:S(2)}, u32[]{:S(2)}) async-start(bf16[64,160,128]{2,1,0:T(8,128)(2,1)} %bitcast.7), calls=%async_computation.2 | async-start | bytes 5242880 | tf_op jit(solution)/shard_map/all_to_all | solution.py:133
  86.8 14.7 %collective-permute-start.3 = (bf16[512,512]{1,0:T(8,128)(2,1)}, bf16[512,512]{1,0:T(8,128)(2,1)}, u32[]{:S(2)}, u32[]{:S(2)}) collective-permute-start(bf16[512,512]{1,0:T(8,128)(2,1)} %bitcast.5), channel_id=1, source_target_pairs={{0,64},{64,128},{128,192},{192,0},{1,65},{65,129},{129,193},{193,1... | collective-permute-start | bytes 1572872 | tf_op jit(solution)/shard_map/ppermute | solution.py:167
  88.2 2.5 copy-start.6
  88.2 2.5 copy-start.7
  92.3 72.2 %collective-permute-start = (bf16[512,1024]{1,0:T(8,128)(2,1)}, bf16[512,1024]{1,0:T(8,128)(2,1)}, u32[]{:S(2)}, u32[]{:S(2)}) collective-permute-start(bf16[512,1024]{1,0:T(8,128)(2,1)} %get-tuple-element.32), channel_id=1, source_target_pairs={{0,64},{64,128},{128,192},{192,0},{1,65},{65,129},{129,193},{193,1... | collective-permute-start | bytes 3145736 | tf_op jit(solution)/shard_map/ppermute | solution.py:167
  93.6 74.0 %collective-permute-start.1 = (bf16[512,1024]{1,0:T(8,128)(2,1)}, bf16[512,1024]{1,0:T(8,128)(2,1)}, u32[]{:S(2)}, u32[]{:S(2)}) collective-permute-start(bf16[512,1024]{1,0:T(8,128)(2,1)} %get-tuple-element.32), channel_id=1, source_target_pairs={{0,128},{64,192},{128,0},{192,64},{1,129},{65,193},{129,1},{193,65... | collective-permute-start | bytes 3145736 | tf_op jit(solution)/shard_map/ppermute | solution.py:167
  95.0 63.8 %collective-permute-start.4 = (bf16[512,512]{1,0:T(8,128)(2,1)}, bf16[512,512]{1,0:T(8,128)(2,1)}, u32[]{:S(2)}, u32[]{:S(2)}) collective-permute-start(bf16[512,512]{1,0:T(8,128)(2,1)} %bitcast.5), channel_id=1, source_target_pairs={{0,128},{64,192},{128,0},{192,64},{1,129},{65,193},{129,1},{193,65... | collective-permute-start | bytes 1572872 | tf_op jit(solution)/shard_map/ppermute | solution.py:167
  96.5 73.3 %collective-permute-start.2 = (bf16[512,1024]{1,0:T(8,128)(2,1)}, bf16[512,1024]{1,0:T(8,128)(2,1)}, u32[]{:S(2)}, u32[]{:S(2)}) collective-permute-start(bf16[512,1024]{1,0:T(8,128)(2,1)} %get-tuple-element.32), channel_id=1, source_target_pairs={{0,192},{64,0},{128,64},{192,128},{1,193},{65,1},{129,65},{193,129... | collective-permute-start | bytes 3145736 | tf_op jit(solution)/shard_map/ppermute | solution.py:167
  101.5 61.9 %collective-permute-start.5 = (bf16[512,512]{1,0:T(8,128)(2,1)}, bf16[512,512]{1,0:T(8,128)(2,1)}, u32[]{:S(2)}, u32[]{:S(2)}) collective-permute-start(bf16[512,512]{1,0:T(8,128)(2,1)} %bitcast.5), channel_id=1, source_target_pairs={{0,192},{64,0},{128,64},{192,128},{1,193},{65,1},{129,65},{193,129... | collective-permute-start | bytes 1572872 | tf_op jit(solution)/shard_map/ppermute | solution.py:167
  164.5 5.4 %copy-start.3 = (bf16[512,2048]{1,0:T(8,128)(2,1)}, bf16[512,2048]{1,0:T(8,128)(2,1)S(1)}, u32[]{:S(2)}) copy-start(bf16[512,2048]{1,0:T(8,128)(2,1)S(1)} %constant_dynamic-update-slice_fusion) | copy-start | bytes 6291460
  180.6 1.5 copy-start.2
  182.0 1.8 copy-start.4
  182.4 0.8 copy-start.5
  188.6 73.7 %all-to-all-start.1 = ((bf16[64,160,128]{2,1,0:T(8,128)(2,1)}), bf16[64,160,128]{2,1,0:T(8,128)(2,1)S(1)}, u32[]{:S(2)}, u32[]{:S(2)}) async-start(bf16[64,160,128]{2,1,0:T(8,128)(2,1)} %reshape_reshape.10), calls=%async_computation.1 | async-start | bytes 5242880 | tf_op jit(solution)/shard_map/all_to_all | solution.py:133
  205.2 0.8 copy-start.9
  205.2 1.0 copy-start.11
  262.3 97.4 %all-to-all-start.3 = ((bf16[64,160,128]{2,1,0:T(8,128)(2,1)}), bf16[64,160,128]{2,1,0:T(8,128)(2,1)}, u32[]{:S(2)}, u32[]{:S(2)}) async-start(bf16[64,160,128]{2,1,0:T(8,128)(2,1)} %reshape_reshape.11), calls=%async_computation.3 | async-start | bytes 5242880 | tf_op jit(solution)/shard_map/all_to_all | solution.py:133
  268.3 6.5 %copy-start.10 = (bf16[640,512]{1,0:T(8,128)(2,1)S(1)}, bf16[640,512]{1,0:T(8,128)(2,1)}, u32[]{:S(2)}) copy-start(bf16[640,512]{1,0:T(8,128)(2,1)} %copy-done.9) | copy-start | bytes 1966084
  268.3 6.5 %copy-start.12 = (bf16[640,512]{1,0:T(8,128)(2,1)S(1)}, bf16[640,512]{1,0:T(8,128)(2,1)}, u32[]{:S(2)}) copy-start(bf16[640,512]{1,0:T(8,128)(2,1)} %copy-done.11) | copy-start | bytes 1966084
  272.2 2.6 copy-start.1
  272.4 14.0 %collective-permute-start.11 = (bf16[512,512]{1,0:T(8,128)(2,1)S(1)}, bf16[512,512]{1,0:T(8,128)(2,1)S(1)}, u32[]{:S(2)}, u32[]{:S(2)}) collective-permute-start(bf16[512,512]{1,0:T(8,128)(2,1)S(1)} %get-tuple-element.28), channel_id=1, source_target_pairs={{0,192},{64,0},{128,64},{192,128},{1,193},{65,1},{129,65},{193,129... | collective-permute-start | bytes 1572872 | tf_op jit(solution)/shard_map/ppermute | solution.py:167
  279.0 74.3 %collective-permute-start.8 = (bf16[512,1024]{1,0:T(8,128)(2,1)S(1)}, bf16[512,1024]{1,0:T(8,128)(2,1)S(1)}, u32[]{:S(2)}, u32[]{:S(2)}) collective-permute-start(bf16[512,1024]{1,0:T(8,128)(2,1)S(1)} %get-tuple-element.23), channel_id=1, source_target_pairs={{0,192},{64,0},{128,64},{192,128},{1,193},{65,1},{129,65},{193,129... | collective-permute-start | bytes 3145736 | tf_op jit(solution)/shard_map/ppermute | solution.py:167
  280.5 72.8 %collective-permute-start.7 = (bf16[512,1024]{1,0:T(8,128)(2,1)S(1)}, bf16[512,1024]{1,0:T(8,128)(2,1)S(1)}, u32[]{:S(2)}, u32[]{:S(2)}) collective-permute-start(bf16[512,1024]{1,0:T(8,128)(2,1)S(1)} %get-tuple-element.24), channel_id=1, source_target_pairs={{0,128},{64,192},{128,0},{192,64},{1,129},{65,193},{129,1},{193,65... | collective-permute-start | bytes 3145736 | tf_op jit(solution)/shard_map/ppermute | solution.py:167
  282.0 71.4 %collective-permute-start.6 = (bf16[512,1024]{1,0:T(8,128)(2,1)S(1)}, bf16[512,1024]{1,0:T(8,128)(2,1)S(1)}, u32[]{:S(2)}, u32[]{:S(2)}) collective-permute-start(bf16[512,1024]{1,0:T(8,128)(2,1)S(1)} %get-tuple-element.22), channel_id=1, source_target_pairs={{0,64},{64,128},{128,192},{192,0},{1,65},{65,129},{129,193},{193,1... | collective-permute-start | bytes 3145736 | tf_op jit(solution)/shard_map/ppermute | solution.py:167
  282.0 57.8 %collective-permute-start.10 = (bf16[512,512]{1,0:T(8,128)(2,1)S(1)}, bf16[512,512]{1,0:T(8,128)(2,1)S(1)}, u32[]{:S(2)}, u32[]{:S(2)}) collective-permute-start(bf16[512,512]{1,0:T(8,128)(2,1)S(1)} %get-tuple-element.29), channel_id=1, source_target_pairs={{0,128},{64,192},{128,0},{192,64},{1,129},{65,193},{129,1},{193,65... | collective-permute-start | bytes 1572872 | tf_op jit(solution)/shard_map/ppermute | solution.py:167
  286.3 65.7 %collective-permute-start.9 = (bf16[512,512]{1,0:T(8,128)(2,1)S(1)}, bf16[512,512]{1,0:T(8,128)(2,1)S(1)}, u32[]{:S(2)}, u32[]{:S(2)}) collective-permute-start(bf16[512,512]{1,0:T(8,128)(2,1)S(1)} %get-tuple-element.27), channel_id=1, source_target_pairs={{0,64},{64,128},{128,192},{192,0},{1,65},{65,129},{129,193},{193,1... | collective-permute-start | bytes 1572872 | tf_op jit(solution)/shard_map/ppermute | solution.py:167

commit v4 on v3

--- a/solution.py
+++ b/solution.py
@@ -20,7 +20,7 @@
     return pl.BlockSpec(memory_space=pltpu.VMEM)
 
 
-def clear_rows(out_ref, step=16):
+def clear_rows(out_ref, step=80):
     rows = out_ref.shape[0]
     zero = jnp.zeros((step,) + out_ref.shape[1:], out_ref.dtype)
 
@@ -40,7 +40,7 @@
     lax.fori_loop(0, count // unroll, step, 0)
 
 
-def route_kernel(capacity, experts, ids_ref, tok_ref, out_ref, pos_ref, place_ref, sem):
+def route_kernel(capacity, experts, ids_ref, tok_ref, out_ref, pos_ref, place_ref, tile_ref, sem):
     top, rows = ids_ref.shape
     f32 = jnp.float32
     expert = lax.broadcasted_iota(jnp.int32, (experts, rows), 0)
@@ -56,15 +56,16 @@
         pos_ref[pl.ds(k, 1), :] = chosen.astype(jnp.int32)
     copy = pltpu.make_async_copy(pos_ref, place_ref, sem)
     copy.start()
+    tile_ref[...] = tok_ref[...].reshape(tile_ref.shape)
     clear_rows(out_ref)
     copy.wait()
 
     def body(t):
-        row = tok_ref[t]
+        row = tile_ref[t]
         for k in range(top):
             out_ref[place_ref[k, t]] = row
 
-    for_each(rows, body)
+    for_each(rows, body, 16)
 
 
 def weigh_kernel(top, pos_ref, gate_ref, cot_ref, out_ref):
@@ -95,14 +96,15 @@
     lax.fori_loop(0, cot_ref.shape[0], body, 0)
 
 
-def gather_sum_kernel(top, pos_ref, back_ref, out_ref):
+def gather_sum_kernel(top, pos_ref, back_ref, out_ref, tile_ref):
     def body(t):
         total = back_ref[pos_ref[0, t]].astype(jnp.float32)
         for k in range(1, top):
             total = total + back_ref[pos_ref[k, t]].astype(jnp.float32)
-        out_ref[t] = total.astype(jnp.bfloat16)
-
-    for_each(out_ref.shape[0], body, 8)
+        tile_ref[t] = total.astype(jnp.bfloat16)
+
+    for_each(out_ref.shape[0], body, 16)
+    out_ref[...] = tile_ref[...].reshape(out_ref.shape)
 
 
 def silu_parts(pre_gate):
@@ -138,7 +140,6 @@
     call = functools.partial(pl.pallas_call, compiler_params=params, interpret=INTERPRET)
 
     gates = gate_probs.T.astype(f32)
-    token_tiles = to_wire(tokens, sub)
     cot_tiles = to_wire(cotangent, sub)
 
     token_send, position = call(
@@ -146,9 +147,9 @@
         out_shape=(wire_shape, jax.ShapeDtypeStruct((top, rows), jnp.int32)),
         in_specs=[vmem(), vmem()],
         out_specs=(vmem(), vmem()),
-        scratch_shapes=[pltpu.SMEM((top, rows), jnp.int32), pltpu.SemaphoreType.DMA],
+        scratch_shapes=[pltpu.SMEM((top, rows), jnp.int32), pltpu.VMEM((rows, sub, LANES), bf16), pltpu.SemaphoreType.DMA],
         name="route",
-    )(expert_ids.T, token_tiles)
+    )(expert_ids.T, tokens)
     token_recv = exchange(token_send)
 
     routed_send = call(
@@ -239,14 +240,15 @@
     mixed, back_grad = lax.optimization_barrier((to_rows(mixed, width), back_grad))
     grad_tokens = call(
         functools.partial(gather_sum_kernel, top),
-        out_shape=token_shape,
+        out_shape=jax.ShapeDtypeStruct((rows, width), bf16),
         in_specs=[smem(), vmem()],
         out_specs=vmem(),
+        scratch_shapes=[pltpu.VMEM((rows, sub, LANES), bf16)],
         name="gather_sum",
     )(position, back_grad)
     return (
         mixed,
-        to_rows(grad_tokens, width),
+        grad_tokens,
         grad_gates,
         grad_gate_w,
         grad_up_w,

time: 365 us -> 365 us (level)
  no operation moved by 1% of the time
where the time goes in v4:
time: 365 us; the launch traced here: 364 us
  waiting for transfers between devices  229 us (63%)
  starting transfers between devices  53.4 us (15%)
  local copies, waits for them, and re-layouts  35.9 us (10%)
  matrix products  26.2 us (7%)
  Pallas kernels  13.9 us (4%)
  other arithmetic  4.79 us (1%)
    ppermute x12, waiting for transfers between devices, to_replica(): lax.ppermute(x, 'dp', [(i, (i + step) % replicas) for i in range(replicas)])  127 us
    all_to_all x4, waiting for transfers between devices, exchange(): lax.all_to_all(chunks, 'expert', 0, 0, tiled=True)  101 us
    all_to_all x4, starting transfers between devices, exchange(): lax.all_to_all(chunks, 'expert', 0, 0, tiled=True)  36.3 us
    dot_general x6, matrix products, dot(): return lax.dot_general(a, b, (dims, ((), ())), preferred_element_type=f32)  26.2 us
    ppermute x12, starting transfers between devices, to_replica(): lax.ppermute(x, 'dp', [(i, (i + step) % replicas) for i in range(replicas)])  17.1 us
    dynamic_update_slice x7, local copies, waits for them, and re-layouts, gather_replicas(): full = lax.dynamic_update_slice_in_dim(full, piece, place, axis)  12 us
    another operation x2, local copies, waits for them, and re-layouts, exchange(): chunks = x.reshape(group, capacity * sub, LANES)  8.42 us
    unnamed x30, local copies, waits for them, and re-layouts  7.74 us
  transfers between devices with their start and end apart: 16, of which 8 were waited for; matrix products, arithmetic and copies ran while one was open for 17% of the time, Pallas kernels for 2%

profile of v4, /device:TPU:1, one launch (start us, length us, event | category | flops | bytes accessed | tf_op | source)
XLA Modules:
  0.0 363.9 jit_solution(16104241080636392572)
XLA Ops:
  2.4 3.2 route.1
  5.6 13.0 %all-to-all-start = ((bf16[64,160,128]{2,1,0:T(8,128)(2,1)}), bf16[64,160,128]{2,1,0:T(8,128)(2,1)S(1)}, u32[]{:S(2)}, u32[]{:S(2)}) async-start(bf16[64,160,128]{2,1,0:T(8,128)(2,1)} %bitcast.2), calls=%async_computation | async-start | bytes 5242880 | tf_op jit(solution)/shard_map/all_to_all | solution.py:135
  19.7 4.0 %weigh.1 = bf16[640,16,128]{2,1,0:T(8,128)(2,1)} custom-call(s32[4,128]{1,0:T(4,128)S(1)} %get-tuple-element.14.pos_ref, f32[4,128]{1,0:T(4,128)S(1)} %convert_bitcast_fusion.gate_ref, bf16[128,16,128]{2,1,0:T(8,128)(2,1)S(1)} %bitcast.44), custom_call_target="tpu_custom_call" | custom-call | tf_op jit(solution)/shard_map/weigh/pallas_call | solution.py:155
  23.8 57.0 %all-to-all-done = bf16[64,160,128]{2,1,0:T(8,128)(2,1)S(1)} async-done(((bf16[64,160,128]{2,1,0:T(8,128)(2,1)}), bf16[64,160,128]{2,1,0:T(8,128)(2,1)S(1)}, u32[]{:S(2)}, u32[]{:S(2)}) %all-to-all-start) | async-done | bytes 2621472 | tf_op jit(solution)/shard_map/all_to_all | solution.py:135
  80.8 5.9 %all-to-all-start.2 = ((bf16[64,160,128]{2,1,0:T(8,128)(2,1)}), bf16[64,160,128]{2,1,0:T(8,128)(2,1)}, u32[]{:S(2)}, u32[]{:S(2)}) async-start(bf16[64,160,128]{2,1,0:T(8,128)(2,1)} %bitcast.7), calls=%async_computation.2 | async-start | bytes 5242880 | tf_op jit(solution)/shard_map/all_to_all | solution.py:135
  88.1 2.5 broadcast_in_dim.15
  90.6 1.6 pad_maximum_fusion.1
  94.8 1.6 collective-permute-start.4
  97.8 3.6 collective-permute-done.3
  105.2 53.4 %collective-permute-done.4 = bf16[512,512]{1,0:T(8,128)(2,1)} collective-permute-done((bf16[512,512]{1,0:T(8,128)(2,1)}, bf16[512,512]{1,0:T(8,128)(2,1)}, u32[]{:S(2)}, u32[]{:S(2)}) %collective-permute-start.4) | collective-permute-done | bytes 524320 | tf_op jit(solution)/shard_map/ppermute | solution.py:168
  159.8 3.5 collective-permute-done.5
  164.4 3.0 constant_dynamic-update-slice_fusion.6
  167.4 2.3 constant_dynamic-update-slice_fusion.5
  169.7 2.3 constant_dynamic-update-slice_fusion.4
  172.0 3.1 reshape_reshape.9
  175.0 5.4 %fusion.8 = f32[640,1024]{1,0:T(8,128)S(1)} fusion(bf16[640,2048]{1,0:T(8,128)(2,1)} %reshape_reshape.9, bf16[2048,1024]{1,0:T(8,128)(2,1)} %constant_dynamic-update-slice_fusion.4), kind=kOutput, calls=%fused_computation.38 | convolution fusion | flops 2684354560 | bytes 9437184 | tf_op jit(solution)/shard_map/dot_general | solution.py:197
  185.3 3.2 reshape_reshape.10
  188.5 11.5 %all-to-all-start.1 = ((bf16[64,160,128]{2,1,0:T(8,128)(2,1)}), bf16[64,160,128]{2,1,0:T(8,128)(2,1)S(1)}, u32[]{:S(2)}, u32[]{:S(2)}) async-start(bf16[64,160,128]{2,1,0:T(8,128)(2,1)} %reshape_reshape.10), calls=%async_computation.1 | async-start | bytes 5242880 | tf_op jit(solution)/shard_map/all_to_all | solution.py:135
  200.0 5.1 %multiply_convert_fusion.1 = (bf16[640,512]{1,0:T(8,128)(2,1)S(1)}, bf16[640,512]{1,0:T(8,128)(2,1)S(1)}) fusion(f32[640,1024]{1,0:T(8,128)} %copy-done.3, bf16[512,2048]{1,0:T(8,128)(2,1)} %copy-done.4, bf16[80,8,16,128]{3,2,1,0:T(8,128)(2,1)} %bitcast.20), kind=kOutput, calls=%fused_computation.14 | convolution fusion | flops 1346437120 | bytes 8650752 | tf_op jit(solution)/shard_map/dot_general | solution.py:197
  206.1 6.4 %convolution_convert_fusion.2 = bf16[640,2048]{1,0:T(8,128)(2,1)} fusion(bf16[2048,1024]{1,0:T(8,128)(2,1)} %constant_dynamic-update-slice_fusion.4, bf16[640,512]{1,0:T(8,128)(2,1)S(1)} %get-tuple-element.26, bf16[640,512]{1,0:T(8,128)(2,1)S(1)} %get-tuple-element.25), kind=kOutput, calls=%fused_computation.2 | convolution fusion | flops 2688286720 | bytes 8126464 | tf_op jit(solution)/shard_map/dot_general | solution.py:197
  212.5 5.3 %reshape_reshape.11 = bf16[64,160,128]{2,1,0:T(8,128)(2,1)} reshape(bf16[640,2048]{1,0:T(8,128)(2,1)} %convolution_convert_fusion.2) | data formatting | bytes 5242880 | tf_op jit(solution)/shard_map/reshape;reshape | solution.py:134
  217.8 44.4 %all-to-all-done.1 = bf16[64,160,128]{2,1,0:T(8,128)(2,1)S(1)} async-done(((bf16[64,160,128]{2,1,0:T(8,128)(2,1)}), bf16[64,160,128]{2,1,0:T(8,128)(2,1)S(1)}, u32[]{:S(2)}, u32[]{:S(2)}) %all-to-all-start.1) | async-done | bytes 2621472 | tf_op jit(solution)/shard_map/all_to_all | solution.py:135
  262.2 5.9 %all-to-all-start.3 = ((bf16[64,160,128]{2,1,0:T(8,128)(2,1)}), bf16[64,160,128]{2,1,0:T(8,128)(2,1)}, u32[]{:S(2)}, u32[]{:S(2)}) async-start(bf16[64,160,128]{2,1,0:T(8,128)(2,1)} %reshape_reshape.11), calls=%async_computation.3 | async-start | bytes 5242880 | tf_op jit(solution)/shard_map/all_to_all | solution.py:135
  268.2 3.9 %convolution_convert_fusion.3 = bf16[512,2048]{1,0:T(8,128)(2,1)S(1)} fusion(bf16[640,512]{1,0:T(8,128)(2,1)} %copy-done.6, bf16[80,8,16,128]{3,2,1,0:T(8,128)(2,1)} %bitcast.20), kind=kOutput, calls=%fused_computation.3 | convolution fusion | flops 1343225856 | bytes 5373952 | tf_op jit(solution)/shard_map/dot_general | solution.py:197
  272.3 2.4 collective-permute-start.11
  274.7 3.9 %convolution_convert_fusion = bf16[2048,1024]{1,0:T(8,128)(2,1)S(1)} fusion(bf16[640,2048]{1,0:T(8,128)(2,1)S(1)} %copy-done.2, bf16[640,512]{1,0:T(8,128)(2,1)S(1)} %copy-done.13, bf16[640,512]{1,0:T(8,128)(2,1)S(1)} %copy-done.11), kind=kOutput, calls=%fused_computation | convolution fusion | flops 2689073152 | bytes 8126464 | tf_op jit(solution)/shard_map/dot_general | solution.py:197
  281.8 2.2 collective-permute-start.10
  284.0 2.2 collective-permute-done.11
  287.4 52.2 %collective-permute-done.10 = bf16[512,512]{1,0:T(8,128)(2,1)S(1)} collective-permute-done((bf16[512,512]{1,0:T(8,128)(2,1)S(1)}, bf16[512,512]{1,0:T(8,128)(2,1)S(1)}, u32[]{:S(2)}, u32[]{:S(2)}) %collective-permute-start.10) | collective-permute-done | bytes 524320 | tf_op jit(solution)/shard_map/ppermute | solution.py:168
  339.6 12.3 %collective-permute-done.9 = bf16[512,512]{1,0:T(8,128)(2,1)S(1)} collective-permute-done((bf16[512,512]{1,0:T(8,128)(2,1)S(1)}, bf16[512,512]{1,0:T(8,128)(2,1)S(1)}, u32[]{:S(2)}, u32[]{:S(2)}) %collective-permute-start.9) | collective-permute-done | bytes 524320 | tf_op jit(solution)/shard_map/ppermute | solution.py:168
  355.5 3.2 mix.1
  359.6 3.5 gather_sum.1
  (61 shorter events, 30.1 us)
Async XLA Ops:
  0.6 1.0 copy-start
  1.7 0.7 copy-start.1
  5.5 14.2 %copy-start.9 = (bf16[128,4]{0,1:T(4,128)(2,1)S(1)}, bf16[128,4]{0,1:T(4,128)(2,1)}, u32[]{:S(2)}) copy-start(bf16[128,4]{0,1:T(4,128)(2,1)} %param.10) | copy-start | bytes 3076
  5.6 75.2 %all-to-all-start = ((bf16[64,160,128]{2,1,0:T(8,128)(2,1)}), bf16[64,160,128]{2,1,0:T(8,128)(2,1)S(1)}, u32[]{:S(2)}, u32[]{:S(2)}) async-start(bf16[64,160,128]{2,1,0:T(8,128)(2,1)} %bitcast.2), calls=%async_computation | async-start | bytes 5242880 | tf_op jit(solution)/shard_map/all_to_all | solution.py:135
  80.8 107.7 %all-to-all-start.2 = ((bf16[64,160,128]{2,1,0:T(8,128)(2,1)}), bf16[64,160,128]{2,1,0:T(8,128)(2,1)}, u32[]{:S(2)}, u32[]{:S(2)}) async-start(bf16[64,160,128]{2,1,0:T(8,128)(2,1)} %bitcast.7), calls=%async_computation.2 | async-start | bytes 5242880 | tf_op jit(solution)/shard_map/all_to_all | solution.py:135
  86.7 14.7 %collective-permute-start.3 = (bf16[512,512]{1,0:T(8,128)(2,1)}, bf16[512,512]{1,0:T(8,128)(2,1)}, u32[]{:S(2)}, u32[]{:S(2)}) collective-permute-start(bf16[512,512]{1,0:T(8,128)(2,1)} %bitcast.5), channel_id=1, source_target_pairs={{0,64},{64,128},{128,192},{192,0},{1,65},{65,129},{129,193},{193,1... | collective-permute-start | bytes 1572872 | tf_op jit(solution)/shard_map/ppermute | solution.py:168
  88.1 2.5 copy-start.7
  88.1 2.5 copy-start.8
  92.2 72.2 %collective-permute-start = (bf16[512,1024]{1,0:T(8,128)(2,1)}, bf16[512,1024]{1,0:T(8,128)(2,1)}, u32[]{:S(2)}, u32[]{:S(2)}) collective-permute-start(bf16[512,1024]{1,0:T(8,128)(2,1)} %get-tuple-element.32), channel_id=1, source_target_pairs={{0,64},{64,128},{128,192},{192,0},{1,65},{65,129},{129,193},{193,1... | collective-permute-start | bytes 3145736 | tf_op jit(solution)/shard_map/ppermute | solution.py:168
  93.5 74.0 %collective-permute-start.1 = (bf16[512,1024]{1,0:T(8,128)(2,1)}, bf16[512,1024]{1,0:T(8,128)(2,1)}, u32[]{:S(2)}, u32[]{:S(2)}) collective-permute-start(bf16[512,1024]{1,0:T(8,128)(2,1)} %get-tuple-element.32), channel_id=1, source_target_pairs={{0,128},{64,192},{128,0},{192,64},{1,129},{65,193},{129,1},{193,65... | collective-permute-start | bytes 3145736 | tf_op jit(solution)/shard_map/ppermute | solution.py:168
  94.8 63.8 %collective-permute-start.4 = (bf16[512,512]{1,0:T(8,128)(2,1)}, bf16[512,512]{1,0:T(8,128)(2,1)}, u32[]{:S(2)}, u32[]{:S(2)}) collective-permute-start(bf16[512,512]{1,0:T(8,128)(2,1)} %bitcast.5), channel_id=1, source_target_pairs={{0,128},{64,192},{128,0},{192,64},{1,129},{65,193},{129,1},{193,65... | collective-permute-start | bytes 1572872 | tf_op jit(solution)/shard_map/ppermute | solution.py:168
  96.4 73.3 %collective-permute-start.2 = (bf16[512,1024]{1,0:T(8,128)(2,1)}, bf16[512,1024]{1,0:T(8,128)(2,1)}, u32[]{:S(2)}, u32[]{:S(2)}) collective-permute-start(bf16[512,1024]{1,0:T(8,128)(2,1)} %get-tuple-element.32), channel_id=1, source_target_pairs={{0,192},{64,0},{128,64},{192,128},{1,193},{65,1},{129,65},{193,129... | collective-permute-start | bytes 3145736 | tf_op jit(solution)/shard_map/ppermute | solution.py:168
  101.4 61.9 %collective-permute-start.5 = (bf16[512,512]{1,0:T(8,128)(2,1)}, bf16[512,512]{1,0:T(8,128)(2,1)}, u32[]{:S(2)}, u32[]{:S(2)}) collective-permute-start(bf16[512,512]{1,0:T(8,128)(2,1)} %bitcast.5), channel_id=1, source_target_pairs={{0,192},{64,0},{128,64},{192,128},{1,193},{65,1},{129,65},{193,129... | collective-permute-start | bytes 1572872 | tf_op jit(solution)/shard_map/ppermute | solution.py:168
  164.4 5.3 %copy-start.4 = (bf16[512,2048]{1,0:T(8,128)(2,1)}, bf16[512,2048]{1,0:T(8,128)(2,1)S(1)}, u32[]{:S(2)}) copy-start(bf16[512,2048]{1,0:T(8,128)(2,1)S(1)} %constant_dynamic-update-slice_fusion) | copy-start | bytes 6291460
  180.5 1.5 copy-start.3
  181.9 1.8 copy-start.5
  182.3 0.8 copy-start.6
  188.5 73.7 %all-to-all-start.1 = ((bf16[64,160,128]{2,1,0:T(8,128)(2,1)}), bf16[64,160,128]{2,1,0:T(8,128)(2,1)S(1)}, u32[]{:S(2)}, u32[]{:S(2)}) async-start(bf16[64,160,128]{2,1,0:T(8,128)(2,1)} %reshape_reshape.10), calls=%async_computation.1 | async-start | bytes 5242880 | tf_op jit(solution)/shard_map/all_to_all | solution.py:135
  205.1 0.8 copy-start.10
  205.1 1.0 copy-start.12
  262.2 97.4 %all-to-all-start.3 = ((bf16[64,160,128]{2,1,0:T(8,128)(2,1)}), bf16[64,160,128]{2,1,0:T(8,128)(2,1)}, u32[]{:S(2)}, u32[]{:S(2)}) async-start(bf16[64,160,128]{2,1,0:T(8,128)(2,1)} %reshape_reshape.11), calls=%async_computation.3 | async-start | bytes 5242880 | tf_op jit(solution)/shard_map/all_to_all | solution.py:135
  268.1 6.5 %copy-start.11 = (bf16[640,512]{1,0:T(8,128)(2,1)S(1)}, bf16[640,512]{1,0:T(8,128)(2,1)}, u32[]{:S(2)}) copy-start(bf16[640,512]{1,0:T(8,128)(2,1)} %copy-done.10) | copy-start | bytes 1966084
  268.2 6.5 %copy-start.13 = (bf16[640,512]{1,0:T(8,128)(2,1)S(1)}, bf16[640,512]{1,0:T(8,128)(2,1)}, u32[]{:S(2)}) copy-start(bf16[640,512]{1,0:T(8,128)(2,1)} %copy-done.12) | copy-start | bytes 1966084
  272.1 2.6 copy-start.2
  272.3 13.9 %collective-permute-start.11 = (bf16[512,512]{1,0:T(8,128)(2,1)S(1)}, bf16[512,512]{1,0:T(8,128)(2,1)S(1)}, u32[]{:S(2)}, u32[]{:S(2)}) collective-permute-start(bf16[512,512]{1,0:T(8,128)(2,1)S(1)} %get-tuple-element.28), channel_id=1, source_target_pairs={{0,192},{64,0},{128,64},{192,128},{1,193},{65,1},{129,65},{193,129... | collective-permute-start | bytes 1572872 | tf_op jit(solution)/shard_map/ppermute | solution.py:168
  278.9 74.3 %collective-permute-start.8 = (bf16[512,1024]{1,0:T(8,128)(2,1)S(1)}, bf16[512,1024]{1,0:T(8,128)(2,1)S(1)}, u32[]{:S(2)}, u32[]{:S(2)}) collective-permute-start(bf16[512,1024]{1,0:T(8,128)(2,1)S(1)} %get-tuple-element.23), channel_id=1, source_target_pairs={{0,192},{64,0},{128,64},{192,128},{1,193},{65,1},{129,65},{193,129... | collective-permute-start | bytes 3145736 | tf_op jit(solution)/shard_map/ppermute | solution.py:168
  280.4 72.8 %collective-permute-start.7 = (bf16[512,1024]{1,0:T(8,128)(2,1)S(1)}, bf16[512,1024]{1,0:T(8,128)(2,1)S(1)}, u32[]{:S(2)}, u32[]{:S(2)}) collective-permute-start(bf16[512,1024]{1,0:T(8,128)(2,1)S(1)} %get-tuple-element.24), channel_id=1, source_target_pairs={{0,128},{64,192},{128,0},{192,64},{1,129},{65,193},{129,1},{193,65... | collective-permute-start | bytes 3145736 | tf_op jit(solution)/shard_map/ppermute | solution.py:168
  281.8 71.4 %collective-permute-start.6 = (bf16[512,1024]{1,0:T(8,128)(2,1)S(1)}, bf16[512,1024]{1,0:T(8,128)(2,1)S(1)}, u32[]{:S(2)}, u32[]{:S(2)}) collective-permute-start(bf16[512,1024]{1,0:T(8,128)(2,1)S(1)} %get-tuple-element.22), channel_id=1, source_target_pairs={{0,64},{64,128},{128,192},{192,0},{1,65},{65,129},{129,193},{193,1... | collective-permute-start | bytes 3145736 | tf_op jit(solution)/shard_map/ppermute | solution.py:168
  281.8 57.8 %collective-permute-start.10 = (bf16[512,512]{1,0:T(8,128)(2,1)S(1)}, bf16[512,512]{1,0:T(8,128)(2,1)S(1)}, u32[]{:S(2)}, u32[]{:S(2)}) collective-permute-start(bf16[512,512]{1,0:T(8,128)(2,1)S(1)} %get-tuple-element.29), channel_id=1, source_target_pairs={{0,128},{64,192},{128,0},{192,64},{1,129},{65,193},{129,1},{193,65... | collective-permute-start | bytes 1572872 | tf_op jit(solution)/shard_map/ppermute | solution.py:168
  286.2 65.7 %collective-permute-start.9 = (bf16[512,512]{1,0:T(8,128)(2,1)S(1)}, bf16[512,512]{1,0:T(8,128)(2,1)S(1)}, u32[]{:S(2)}, u32[]{:S(2)}) collective-permute-start(bf16[512,512]{1,0:T(8,128)(2,1)S(1)} %get-tuple-element.27), channel_id=1, source_target_pairs={{0,64},{64,128},{128,192},{192,0},{1,65},{65,129},{129,193},{193,1... | collective-permute-start | bytes 1572872 | tf_op jit(solution)/shard_map/ppermute | solution.py:168

commit v5 on v4

--- a/solution.py
+++ b/solution.py
@@ -97,10 +97,12 @@
 
 
 def gather_sum_kernel(top, pos_ref, back_ref, out_ref, tile_ref):
+    base = pl.program_id(0) * out_ref.shape[0]
+
     def body(t):
-        total = back_ref[pos_ref[0, t]].astype(jnp.float32)
+        total = back_ref[pos_ref[0, base + t]].astype(jnp.float32)
         for k in range(1, top):
-            total = total + back_ref[pos_ref[k, t]].astype(jnp.float32)
+            total = total + back_ref[pos_ref[k, base + t]].astype(jnp.float32)
         tile_ref[t] = total.astype(jnp.bfloat16)
 
     for_each(out_ref.shape[0], body, 16)
@@ -238,12 +240,14 @@
     grad_gates = jnp.sum(dots, axis=1).reshape(top, rows).T
 
     mixed, back_grad = lax.optimization_barrier((to_rows(mixed, width), back_grad))
+    part = rows // 4 if rows % 64 == 0 else rows
     grad_tokens = call(
         functools.partial(gather_sum_kernel, top),
         out_shape=jax.ShapeDtypeStruct((rows, width), bf16),
+        grid=(rows // part,),
         in_specs=[smem(), vmem()],
-        out_specs=vmem(),
-        scratch_shapes=[pltpu.VMEM((rows, sub, LANES), bf16)],
+        out_specs=pl.BlockSpec((part, width), lambda i: (i, 0)),
+        scratch_shapes=[pltpu.VMEM((part, sub, LANES), bf16)],
         name="gather_sum",
     )(position, back_grad)
     return (

time: 365 us -> 365 us (level)
  no operation moved by 1% of the time
where the time goes in v5:
time: 365 us; the launch traced here: 364 us
  waiting for transfers between devices  229 us (63%)
  starting transfers between devices  53.4 us (15%)
  local copies, waits for them, and re-layouts  35.9 us (10%)
  matrix products  26.2 us (7%)
  Pallas kernels  14.3 us (4%)
  other arithmetic  4.79 us (1%)
    ppermute x12, waiting for transfers between devices, to_replica(): lax.ppermute(x, 'dp', [(i, (i + step) % replicas) for i in range(replicas)])  127 us
    all_to_all x4, waiting for transfers between devices, exchange(): lax.all_to_all(chunks, 'expert', 0, 0, tiled=True)  101 us
    all_to_all x4, starting transfers between devices, exchange(): lax.all_to_all(chunks, 'expert', 0, 0, tiled=True)  36.3 us
    dot_general x6, matrix products, dot(): return lax.dot_general(a, b, (dims, ((), ())), preferred_element_type=f32)  26.2 us
    ppermute x12, starting transfers between devices, to_replica(): lax.ppermute(x, 'dp', [(i, (i + step) % replicas) for i in range(replicas)])  17.1 us
    dynamic_update_slice x7, local copies, waits for them, and re-layouts, gather_replicas(): full = lax.dynamic_update_slice_in_dim(full, piece, place, axis)  12 us
    another operation x2, local copies, waits for them, and re-layouts, exchange(): chunks = x.reshape(group, capacity * sub, LANES)  8.42 us
    unnamed x30, local copies, waits for them, and re-layouts  7.74 us
  transfers between devices with their start and end apart: 16, of which 8 were waited for; matrix products, arithmetic and copies ran while one was open for 17% of the time, Pallas kernels for 2%

profile of v5, /device:TPU:1, one launch (start us, length us, event | category | flops | bytes accessed | tf_op | source)
XLA Modules:
  0.0 364.2 jit_solution(13724927198879163020)
XLA Ops:
  2.4 3.2 route.1
  5.6 13.0 %all-to-all-start = ((bf16[64,160,128]{2,1,0:T(8,128)(2,1)}), bf16[64,160,128]{2,1,0:T(8,128)(2,1)S(1)}, u32[]{:S(2)}, u32[]{:S(2)}) async-start(bf16[64,160,128]{2,1,0:T(8,128)(2,1)} %bitcast.2), calls=%async_computation | async-start | bytes 5242880 | tf_op jit(solution)/shard_map/all_to_all | solution.py:137
  19.7 4.0 %weigh.1 = bf16[640,16,128]{2,1,0:T(8,128)(2,1)} custom-call(s32[4,128]{1,0:T(4,128)S(1)} %get-tuple-element.14.pos_ref, f32[4,128]{1,0:T(4,128)S(1)} %convert_bitcast_fusion.gate_ref, bf16[128,16,128]{2,1,0:T(8,128)(2,1)S(1)} %bitcast.44), custom_call_target="tpu_custom_call" | custom-call | tf_op jit(solution)/shard_map/weigh/pallas_call | solution.py:157
  23.8 57.0 %all-to-all-done = bf16[64,160,128]{2,1,0:T(8,128)(2,1)S(1)} async-done(((bf16[64,160,128]{2,1,0:T(8,128)(2,1)}), bf16[64,160,128]{2,1,0:T(8,128)(2,1)S(1)}, u32[]{:S(2)}, u32[]{:S(2)}) %all-to-all-start) | async-done | bytes 2621472 | tf_op jit(solution)/shard_map/all_to_all | solution.py:137
  80.8 5.9 %all-to-all-start.2 = ((bf16[64,160,128]{2,1,0:T(8,128)(2,1)}), bf16[64,160,128]{2,1,0:T(8,128)(2,1)}, u32[]{:S(2)}, u32[]{:S(2)}) async-start(bf16[64,160,128]{2,1,0:T(8,128)(2,1)} %bitcast.7), calls=%async_computation.2 | async-start | bytes 5242880 | tf_op jit(solution)/shard_map/all_to_all | solution.py:137
  88.1 2.5 broadcast_in_dim.15
  90.6 1.6 pad_maximum_fusion.1
  94.8 1.6 collective-permute-start.4
  97.8 3.6 collective-permute-done.3
  105.2 53.4 %collective-permute-done.4 = bf16[512,512]{1,0:T(8,128)(2,1)} collective-permute-done((bf16[512,512]{1,0:T(8,128)(2,1)}, bf16[512,512]{1,0:T(8,128)(2,1)}, u32[]{:S(2)}, u32[]{:S(2)}) %collective-permute-start.4) | collective-permute-done | bytes 524320 | tf_op jit(solution)/shard_map/ppermute | solution.py:170
  159.8 3.5 collective-permute-done.5
  164.4 3.0 constant_dynamic-update-slice_fusion.6
  167.4 2.3 constant_dynamic-update-slice_fusion.5
  169.7 2.3 constant_dynamic-update-slice_fusion.4
  172.0 3.1 reshape_reshape.9
  175.0 5.4 %fusion.8 = f32[640,1024]{1,0:T(8,128)S(1)} fusion(bf16[640,2048]{1,0:T(8,128)(2,1)} %reshape_reshape.9, bf16[2048,1024]{1,0:T(8,128)(2,1)} %constant_dynamic-update-slice_fusion.4), kind=kOutput, calls=%fused_computation.38 | convolution fusion | flops 2684354560 | bytes 9437184 | tf_op jit(solution)/shard_map/dot_general | solution.py:199
  185.3 3.2 reshape_reshape.10
  188.5 11.5 %all-to-all-start.1 = ((bf16[64,160,128]{2,1,0:T(8,128)(2,1)}), bf16[64,160,128]{2,1,0:T(8,128)(2,1)S(1)}, u32[]{:S(2)}, u32[]{:S(2)}) async-start(bf16[64,160,128]{2,1,0:T(8,128)(2,1)} %reshape_reshape.10), calls=%async_computation.1 | async-start | bytes 5242880 | tf_op jit(solution)/shard_map/all_to_all | solution.py:137
  200.0 5.1 %multiply_convert_fusion.1 = (bf16[640,512]{1,0:T(8,128)(2,1)S(1)}, bf16[640,512]{1,0:T(8,128)(2,1)S(1)}) fusion(f32[640,1024]{1,0:T(8,128)} %copy-done.3, bf16[512,2048]{1,0:T(8,128)(2,1)} %copy-done.4, bf16[80,8,16,128]{3,2,1,0:T(8,128)(2,1)} %bitcast.20), kind=kOutput, calls=%fused_computation.14 | convolution fusion | flops 1346437120 | bytes 8650752 | tf_op jit(solution)/shard_map/dot_general | solution.py:199
  206.1 6.4 %convolution_convert_fusion.2 = bf16[640,2048]{1,0:T(8,128)(2,1)} fusion(bf16[2048,1024]{1,0:T(8,128)(2,1)} %constant_dynamic-update-slice_fusion.4, bf16[640,512]{1,0:T(8,128)(2,1)S(1)} %get-tuple-element.26, bf16[640,512]{1,0:T(8,128)(2,1)S(1)} %get-tuple-element.25), kind=kOutput, calls=%fused_computation.2 | convolution fusion | flops 2688286720 | bytes 8126464 | tf_op jit(solution)/shard_map/dot_general | solution.py:199
  212.5 5.3 %reshape_reshape.11 = bf16[64,160,128]{2,1,0:T(8,128)(2,1)} reshape(bf16[640,2048]{1,0:T(8,128)(2,1)} %convolution_convert_fusion.2) | data formatting | bytes 5242880 | tf_op jit(solution)/shard_map/reshape;reshape | solution.py:136
  217.8 44.4 %all-to-all-done.1 = bf16[64,160,128]{2,1,0:T(8,128)(2,1)S(1)} async-done(((bf16[64,160,128]{2,1,0:T(8,128)(2,1)}), bf16[64,160,128]{2,1,0:T(8,128)(2,1)S(1)}, u32[]{:S(2)}, u32[]{:S(2)}) %all-to-all-start.1) | async-done | bytes 2621472 | tf_op jit(solution)/shard_map/all_to_all | solution.py:137
  262.2 5.9 %all-to-all-start.3 = ((bf16[64,160,128]{2,1,0:T(8,128)(2,1)}), bf16[64,160,128]{2,1,0:T(8,128)(2,1)}, u32[]{:S(2)}, u32[]{:S(2)}) async-start(bf16[64,160,128]{2,1,0:T(8,128)(2,1)} %reshape_reshape.11), calls=%async_computation.3 | async-start | bytes 5242880 | tf_op jit(solution)/shard_map/all_to_all | solution.py:137
  268.2 3.9 %convolution_convert_fusion.3 = bf16[512,2048]{1,0:T(8,128)(2,1)S(1)} fusion(bf16[640,512]{1,0:T(8,128)(2,1)} %copy-done.6, bf16[80,8,16,128]{3,2,1,0:T(8,128)(2,1)} %bitcast.20), kind=kOutput, calls=%fused_computation.3 | convolution fusion | flops 1343225856 | bytes 5373952 | tf_op jit(solution)/shard_map/dot_general | solution.py:199
  272.3 2.4 collective-permute-start.11
  274.7 3.9 %convolution_convert_fusion = bf16[2048,1024]{1,0:T(8,128)(2,1)S(1)} fusion(bf16[640,2048]{1,0:T(8,128)(2,1)S(1)} %copy-done.2, bf16[640,512]{1,0:T(8,128)(2,1)S(1)} %copy-done.13, bf16[640,512]{1,0:T(8,128)(2,1)S(1)} %copy-done.11), kind=kOutput, calls=%fused_computation | convolution fusion | flops 2689073152 | bytes 8126464 | tf_op jit(solution)/shard_map/dot_general | solution.py:199
  281.8 2.2 collective-permute-start.10
  284.0 2.2 collective-permute-done.11
  287.4 52.2 %collective-permute-done.10 = bf16[512,512]{1,0:T(8,128)(2,1)S(1)} collective-permute-done((bf16[512,512]{1,0:T(8,128)(2,1)S(1)}, bf16[512,512]{1,0:T(8,128)(2,1)S(1)}, u32[]{:S(2)}, u32[]{:S(2)}) %collective-permute-start.10) | collective-permute-done | bytes 524320 | tf_op jit(solution)/shard_map/ppermute | solution.py:170
  339.6 12.3 %collective-permute-done.9 = bf16[512,512]{1,0:T(8,128)(2,1)S(1)} collective-permute-done((bf16[512,512]{1,0:T(8,128)(2,1)S(1)}, bf16[512,512]{1,0:T(8,128)(2,1)S(1)}, u32[]{:S(2)}, u32[]{:S(2)}) %collective-permute-start.9) | collective-permute-done | bytes 524320 | tf_op jit(solution)/shard_map/ppermute | solution.py:170
  355.5 3.2 mix.1
  359.6 3.9 %gather_sum.1 = bf16[128,2048]{1,0:T(8,128)(2,1)} custom-call(s32[4,128]{1,0:T(4,128)S(1)} %get-tuple-element.14.pos_ref, bf16[640,16,128]{2,1,0:T(8,128)(2,1)} %bitcast.9.back_ref), custom_call_target="tpu_custom_call" | custom-call | tf_op jit(solution)/shard_map/gather_sum/pallas_call | solution.py:244
  (61 shorter events, 30.1 us)
Async XLA Ops:
  0.6 1.0 copy-start
  1.7 0.7 copy-start.1
  5.5 14.2 %copy-start.9 = (bf16[128,4]{0,1:T(4,128)(2,1)S(1)}, bf16[128,4]{0,1:T(4,128)(2,1)}, u32[]{:S(2)}) copy-start(bf16[128,4]{0,1:T(4,128)(2,1)} %param.10) | copy-start | bytes 3076
  5.6 75.2 %all-to-all-start = ((bf16[64,160,128]{2,1,0:T(8,128)(2,1)}), bf16[64,160,128]{2,1,0:T(8,128)(2,1)S(1)}, u32[]{:S(2)}, u32[]{:S(2)}) async-start(bf16[64,160,128]{2,1,0:T(8,128)(2,1)} %bitcast.2), calls=%async_computation | async-start | bytes 5242880 | tf_op jit(solution)/shard_map/all_to_all | solution.py:137
  80.8 107.7 %all-to-all-start.2 = ((bf16[64,160,128]{2,1,0:T(8,128)(2,1)}), bf16[64,160,128]{2,1,0:T(8,128)(2,1)}, u32[]{:S(2)}, u32[]{:S(2)}) async-start(bf16[64,160,128]{2,1,0:T(8,128)(2,1)} %bitcast.7), calls=%async_computation.2 | async-start | bytes 5242880 | tf_op jit(solution)/shard_map/all_to_all | solution.py:137
  86.7 14.7 %collective-permute-start.3 = (bf16[512,512]{1,0:T(8,128)(2,1)}, bf16[512,512]{1,0:T(8,128)(2,1)}, u32[]{:S(2)}, u32[]{:S(2)}) collective-permute-start(bf16[512,512]{1,0:T(8,128)(2,1)} %bitcast.5), channel_id=1, source_target_pairs={{0,64},{64,128},{128,192},{192,0},{1,65},{65,129},{129,193},{193,1... | collective-permute-start | bytes 1572872 | tf_op jit(solution)/shard_map/ppermute | solution.py:170
  88.1 2.5 copy-start.7
  88.1 2.5 copy-start.8
  92.2 72.2 %collective-permute-start = (bf16[512,1024]{1,0:T(8,128)(2,1)}, bf16[512,1024]{1,0:T(8,128)(2,1)}, u32[]{:S(2)}, u32[]{:S(2)}) collective-permute-start(bf16[512,1024]{1,0:T(8,128)(2,1)} %get-tuple-element.32), channel_id=1, source_target_pairs={{0,64},{64,128},{128,192},{192,0},{1,65},{65,129},{129,193},{193,1... | collective-permute-start | bytes 3145736 | tf_op jit(solution)/shard_map/ppermute | solution.py:170
  93.5 74.0 %collective-permute-start.1 = (bf16[512,1024]{1,0:T(8,128)(2,1)}, bf16[512,1024]{1,0:T(8,128)(2,1)}, u32[]{:S(2)}, u32[]{:S(2)}) collective-permute-start(bf16[512,1024]{1,0:T(8,128)(2,1)} %get-tuple-element.32), channel_id=1, source_target_pairs={{0,128},{64,192},{128,0},{192,64},{1,129},{65,193},{129,1},{193,65... | collective-permute-start | bytes 3145736 | tf_op jit(solution)/shard_map/ppermute | solution.py:170
  94.8 63.8 %collective-permute-start.4 = (bf16[512,512]{1,0:T(8,128)(2,1)}, bf16[512,512]{1,0:T(8,128)(2,1)}, u32[]{:S(2)}, u32[]{:S(2)}) collective-permute-start(bf16[512,512]{1,0:T(8,128)(2,1)} %bitcast.5), channel_id=1, source_target_pairs={{0,128},{64,192},{128,0},{192,64},{1,129},{65,193},{129,1},{193,65... | collective-permute-start | bytes 1572872 | tf_op jit(solution)/shard_map/ppermute | solution.py:170
  96.4 73.3 %collective-permute-start.2 = (bf16[512,1024]{1,0:T(8,128)(2,1)}, bf16[512,1024]{1,0:T(8,128)(2,1)}, u32[]{:S(2)}, u32[]{:S(2)}) collective-permute-start(bf16[512,1024]{1,0:T(8,128)(2,1)} %get-tuple-element.32), channel_id=1, source_target_pairs={{0,192},{64,0},{128,64},{192,128},{1,193},{65,1},{129,65},{193,129... | collective-permute-start | bytes 3145736 | tf_op jit(solution)/shard_map/ppermute | solution.py:170
  101.4 61.9 %collective-permute-start.5 = (bf16[512,512]{1,0:T(8,128)(2,1)}, bf16[512,512]{1,0:T(8,128)(2,1)}, u32[]{:S(2)}, u32[]{:S(2)}) collective-permute-start(bf16[512,512]{1,0:T(8,128)(2,1)} %bitcast.5), channel_id=1, source_target_pairs={{0,192},{64,0},{128,64},{192,128},{1,193},{65,1},{129,65},{193,129... | collective-permute-start | bytes 1572872 | tf_op jit(solution)/shard_map/ppermute | solution.py:170
  164.4 5.3 %copy-start.4 = (bf16[512,2048]{1,0:T(8,128)(2,1)}, bf16[512,2048]{1,0:T(8,128)(2,1)S(1)}, u32[]{:S(2)}) copy-start(bf16[512,2048]{1,0:T(8,128)(2,1)S(1)} %constant_dynamic-update-slice_fusion) | copy-start | bytes 6291460
  180.5 1.5 copy-start.3
  181.9 1.8 copy-start.5
  182.3 0.8 copy-start.6
  188.5 73.7 %all-to-all-start.1 = ((bf16[64,160,128]{2,1,0:T(8,128)(2,1)}), bf16[64,160,128]{2,1,0:T(8,128)(2,1)S(1)}, u32[]{:S(2)}, u32[]{:S(2)}) async-start(bf16[64,160,128]{2,1,0:T(8,128)(2,1)} %reshape_reshape.10), calls=%async_computation.1 | async-start | bytes 5242880 | tf_op jit(solution)/shard_map/all_to_all | solution.py:137
  205.1 0.8 copy-start.10
  205.1 1.0 copy-start.12
  262.2 97.4 %all-to-all-start.3 = ((bf16[64,160,128]{2,1,0:T(8,128)(2,1)}), bf16[64,160,128]{2,1,0:T(8,128)(2,1)}, u32[]{:S(2)}, u32[]{:S(2)}) async-start(bf16[64,160,128]{2,1,0:T(8,128)(2,1)} %reshape_reshape.11), calls=%async_computation.3 | async-start | bytes 5242880 | tf_op jit(solution)/shard_map/all_to_all | solution.py:137
  268.1 6.5 %copy-start.11 = (bf16[640,512]{1,0:T(8,128)(2,1)S(1)}, bf16[640,512]{1,0:T(8,128)(2,1)}, u32[]{:S(2)}) copy-start(bf16[640,512]{1,0:T(8,128)(2,1)} %copy-done.10) | copy-start | bytes 1966084
  268.2 6.5 %copy-start.13 = (bf16[640,512]{1,0:T(8,128)(2,1)S(1)}, bf16[640,512]{1,0:T(8,128)(2,1)}, u32[]{:S(2)}) copy-start(bf16[640,512]{1,0:T(8,128)(2,1)} %copy-done.12) | copy-start | bytes 1966084
  272.1 2.6 copy-start.2
  272.3 13.9 %collective-permute-start.11 = (bf16[512,512]{1,0:T(8,128)(2,1)S(1)}, bf16[512,512]{1,0:T(8,128)(2,1)S(1)}, u32[]{:S(2)}, u32[]{:S(2)}) collective-permute-start(bf16[512,512]{1,0:T(8,128)(2,1)S(1)} %get-tuple-element.28), channel_id=1, source_target_pairs={{0,192},{64,0},{128,64},{192,128},{1,193},{65,1},{129,65},{193,129... | collective-permute-start | bytes 1572872 | tf_op jit(solution)/shard_map/ppermute | solution.py:170
  278.9 74.3 %collective-permute-start.8 = (bf16[512,1024]{1,0:T(8,128)(2,1)S(1)}, bf16[512,1024]{1,0:T(8,128)(2,1)S(1)}, u32[]{:S(2)}, u32[]{:S(2)}) collective-permute-start(bf16[512,1024]{1,0:T(8,128)(2,1)S(1)} %get-tuple-element.23), channel_id=1, source_target_pairs={{0,192},{64,0},{128,64},{192,128},{1,193},{65,1},{129,65},{193,129... | collective-permute-start | bytes 3145736 | tf_op jit(solution)/shard_map/ppermute | solution.py:170
  280.4 72.8 %collective-permute-start.7 = (bf16[512,1024]{1,0:T(8,128)(2,1)S(1)}, bf16[512,1024]{1,0:T(8,128)(2,1)S(1)}, u32[]{:S(2)}, u32[]{:S(2)}) collective-permute-start(bf16[512,1024]{1,0:T(8,128)(2,1)S(1)} %get-tuple-element.24), channel_id=1, source_target_pairs={{0,128},{64,192},{128,0},{192,64},{1,129},{65,193},{129,1},{193,65... | collective-permute-start | bytes 3145736 | tf_op jit(solution)/shard_map/ppermute | solution.py:170
  281.8 71.4 %collective-permute-start.6 = (bf16[512,1024]{1,0:T(8,128)(2,1)S(1)}, bf16[512,1024]{1,0:T(8,128)(2,1)S(1)}, u32[]{:S(2)}, u32[]{:S(2)}) collective-permute-start(bf16[512,1024]{1,0:T(8,128)(2,1)S(1)} %get-tuple-element.22), channel_id=1, source_target_pairs={{0,64},{64,128},{128,192},{192,0},{1,65},{65,129},{129,193},{193,1... | collective-permute-start | bytes 3145736 | tf_op jit(solution)/shard_map/ppermute | solution.py:170
  281.8 57.8 %collective-permute-start.10 = (bf16[512,512]{1,0:T(8,128)(2,1)S(1)}, bf16[512,512]{1,0:T(8,128)(2,1)S(1)}, u32[]{:S(2)}, u32[]{:S(2)}) collective-permute-start(bf16[512,512]{1,0:T(8,128)(2,1)S(1)} %get-tuple-element.29), channel_id=1, source_target_pairs={{0,128},{64,192},{128,0},{192,64},{1,129},{65,193},{129,1},{193,65... | collective-permute-start | bytes 1572872 | tf_op jit(solution)/shard_map/ppermute | solution.py:170
  286.2 65.7 %collective-permute-start.9 = (bf16[512,512]{1,0:T(8,128)(2,1)S(1)}, bf16[512,512]{1,0:T(8,128)(2,1)S(1)}, u32[]{:S(2)}, u32[]{:S(2)}) collective-permute-start(bf16[512,512]{1,0:T(8,128)(2,1)S(1)} %get-tuple-element.27), channel_id=1, source_target_pairs={{0,64},{64,128},{128,192},{192,0},{1,65},{65,129},{129,193},{193,1... | collective-permute-start | bytes 1572872 | tf_op jit(solution)/shard_map/ppermute | solution.py:170
